TPU v7x, 32 devices: a whole 2x2x4 slice. The times are simulated.
32 devices in a mesh: groups: 2 (over y), seq: 4 (over z), head: 4 (over x, core).
Axes of the slice: x: 2, y: 2, z: 4, core: 2. Of those that a mesh axis runs over, the one named last changes fastest.
Arguments:
- layer_queries: bfloat16 [4096, 4096], P(('groups', 'seq'), 'head'), parts along dimension 0, may hold values from -1.75 to 1.75
- layer_keys: bfloat16 [4096, 4096], P(('groups', 'seq'), 'head'), parts along dimension 0, may hold values from -1.75 to 1.75
- layer_values: bfloat16 [4096, 4096], P(('groups', 'seq'), 'head'), parts along dimension 0, may hold values from -6 to 6
- gate_logits: bfloat16 [4096, 4096], P(('groups', 'seq'), 'head'), parts along dimension 0, may hold values from -6 to 6
- norm_gain: bfloat16 [4096], P('head'), may hold values from 0.099609375 to 1.8984375
- decay_exponents: int32 [32], P('head'), may hold values from 0 to 9
- doc_lengths: int32 [8], P('groups'), parts along dimension 0, may hold values from 1 to 1024, 2048 in all
- out_weight: bfloat16 [6144, 4096], P('seq', 'head'), may hold values from -0.125 to 0.125
Outputs:
- layer_output: bfloat16 [4096, 6144], P(('groups', 'seq'), 'head'), parts along dimension 0
There are 2 independent parts, one for each index of `groups`. A program takes and returns all parts, laid end to end along the dimension named above; an argument that names none is the same for every part. Nothing has to cross between parts.
Inputs may be any that keep to these rules, and one draw needn't show every extreme that they name: `doc_lengths`: the lengths sum to 2048.
All inputs are finite; a program needn't handle non-finite values.
Results may differ from a plain program's by a relative error of at most 0.0063.
Values may be sent and summed in bfloat16 or wider, within the bound.
No kernel may reach another device: no remote copies, remote signals or barrier semaphores. Data moves between devices by JAX's collectives and lax.ppermute only.
A program may use at most 128 MiB of HBM per device.

v0:
```python
import functools

import jax
import jax.numpy as jnp
from jax import lax
from jax.experimental import pallas as pl
from jax.experimental.pallas import tpu as pltpu
from jax.sharding import PartitionSpec as P

HEAD_DIM = 128
NT = (((1,), (1,)), ((), ()))
TN = (((0,), (0,)), ((), ()))
SMEM = pl.BlockSpec(memory_space=pltpu.SMEM)
HBM = pl.BlockSpec(memory_space=pltpu.HBM)
ANY = pl.BlockSpec(memory_space=pl.ANY)
STEPS = 4


def cost(flops, mib):
    return pl.CostEstimate(flops=int(flops), bytes_accessed=int(mib * (1 << 20)), transcendentals=0)


def begin_of(doc_lengths, position):
    count = doc_lengths.shape[0]
    order = jnp.arange(count, dtype=jnp.int32)
    ends = jnp.sum(jnp.where(order[None, :] <= order[:, None], doc_lengths[None, :], 0), axis=1)
    return jnp.sum(jnp.where(ends[None, :] <= position[:, None], doc_lengths[None, :], 0), axis=1)


def attention_parts(layer_queries, layer_keys, layer_values, decay_exponents, doc_lengths):
    tok_rows = layer_queries.shape[0]
    heads_here = decay_exponents.shape[0]
    token_span = tok_rows * lax.axis_size("seq")
    block = lax.axis_index("seq")
    decay_rate = jnp.minimum(jnp.exp2(decay_exponents.astype(jnp.float32)) / token_span, 1.0 / 32.0)
    local_pos = jnp.arange(tok_rows, dtype=jnp.int32)
    position = block * tok_rows + local_pos
    within = position - begin_of(doc_lengths, position)
    query_heads = layer_queries.reshape(tok_rows, heads_here, HEAD_DIM)
    key_heads = layer_keys.reshape(tok_rows, heads_here, HEAD_DIM)
    value_heads = layer_values.reshape(tok_rows, heads_here, HEAD_DIM)

    last_within = within[tok_rows - 1]
    key_weight = jnp.where(
        (local_pos >= tok_rows - 1 - last_within)[:, None],
        jnp.exp(-decay_rate[None, :] * (tok_rows - local_pos)[:, None].astype(jnp.float32)),
        0.0,
    )
    scaled = (key_heads.astype(jnp.float32) * key_weight[:, :, None]).astype(jnp.bfloat16)
    block_state = jnp.einsum(
        "thd,the->hde", scaled, value_heads, preferred_element_type=jnp.float32
    )

    def intra():
        lag_grid = local_pos[:, None] - local_pos[None, :]
        valid_mask = (lag_grid >= 0) & (lag_grid <= within[:, None])
        decay_grid = jnp.where(
            valid_mask[None],
            jnp.exp(-decay_rate[:, None, None] * lag_grid[None].astype(jnp.float32)),
            0.0,
        )
        scores = jnp.einsum(
            "thd,shd->hts", query_heads, key_heads, preferred_element_type=jnp.float32
        )
        weights = (scores * decay_grid).astype(jnp.bfloat16)
        return jnp.einsum("hts,shd->thd", weights, value_heads, preferred_element_type=jnp.float32)

    def cross(incoming):
        query_weight = jnp.where(
            (within >= local_pos + 1)[:, None],
            jnp.exp(-decay_rate[None, :] * local_pos[:, None].astype(jnp.float32)),
            0.0,
        )
        return (
            jnp.einsum(
                "thd,hde->the",
                query_heads,
                incoming.astype(jnp.bfloat16),
                preferred_element_type=jnp.float32,
            )
            * query_weight[:, :, None]
        )

    return decay_rate, block_state, intra, cross


def carry_of(block, decay_rate, doc_lengths, tok_rows):
    last = (block * tok_rows + tok_rows - 1)[None]
    last_within = (last - begin_of(doc_lengths, last))[0]
    return jnp.where(last_within >= tok_rows, jnp.exp(-decay_rate * tok_rows), 0.0)


def limit(mib):
    return pltpu.CompilerParams(vmem_limit_bytes=mib << 20)


def begin_at(docs, position):
    begin, end = 0, 0
    for doc in range(docs.shape[0]):
        end = end + docs[doc]
        begin = jnp.where(position >= end, end, begin)
    return begin


def row_begin(docs, block, rows):
    shape = (rows, HEAD_DIM)
    position = block * rows + lax.broadcasted_iota(jnp.int32, shape, 0)
    begin = jnp.zeros(shape, jnp.int32)
    end = 0
    for doc in range(docs.shape[0]):
        end = end + docs[doc]
        begin = jnp.where(position >= end, end, begin)
    return begin - block * rows


def rate_of(exponents, head, span):
    doubled = lax.shift_left(jnp.int32(1), exponents[head]).astype(jnp.float32)
    return jnp.minimum(doubled * (1.0 / span), 1.0 / 32.0)


def each_head(width):
    here = width // HEAD_DIM
    for n in range(here):
        yield n, pl.program_id(0) * here + n, slice(n * HEAD_DIM, (n + 1) * HEAD_DIM)


def state_kernel(where, docs, exponents, keys, values, state, *, span):
    rows, width = keys.shape
    block = where[0]
    begin = begin_at(docs, block * rows + rows - 1)
    local = lax.broadcasted_iota(jnp.int32, (rows, HEAD_DIM), 0)
    kept = local >= begin - block * rows
    left = (rows - local).astype(jnp.float32)
    for n, head, columns in each_head(width):
        weight = jnp.where(kept, jnp.exp(-rate_of(exponents, head, span) * left), 0.0)
        scaled = (keys[:, columns].astype(jnp.float32) * weight).astype(jnp.bfloat16)
        made = lax.dot_general(scaled, values[:, columns], TN, preferred_element_type=jnp.float32)
        state[n] = made.astype(jnp.bfloat16)


def intra_kernel(where, docs, exponents, queries, keys, values, out, *, span):
    rows, width = queries.shape
    part = rows // 2
    begin = row_begin(docs, where[0], rows)[:, :1]
    for step in range(2):
        low, seen = step * part, (step + 1) * part
        row = low + lax.broadcasted_iota(jnp.int32, (part, seen), 0)
        column = lax.broadcasted_iota(jnp.int32, (part, seen), 1)
        valid = (column <= row) & (column >= begin[low:seen])
        lag = (row - column).astype(jnp.float32)
        for n, head, columns in each_head(width):
            scores = lax.dot_general(
                queries[low:seen, columns], keys[:seen, columns], NT, preferred_element_type=jnp.float32
            )
            decay = jnp.exp(-rate_of(exponents, head, span) * lag)
            weights = jnp.where(valid, scores * decay, 0.0).astype(jnp.bfloat16)
            out[low:seen, columns] = jnp.dot(
                weights, values[:seen, columns], preferred_element_type=jnp.float32
            )


def gate_kernel(
    where, docs, exponents, queries, intra, near, far, gain, gate, out, squares, total, *, span
):
    rows, width = queries.shape
    block = where[0]
    local = lax.broadcasted_iota(jnp.int32, (rows, HEAD_DIM), 0).astype(jnp.float32)
    reaches = row_begin(docs, block, rows) < 0
    whole = begin_at(docs, block * rows - 1) <= (block - 1) * rows - 1

    @pl.when(pl.program_id(0) == 0)
    def _():
        total[...] = jnp.zeros_like(total)

    for n, head, columns in each_head(width):
        rate = rate_of(exponents, head, span)
        weight = jnp.where(reaches, jnp.exp(-rate * local), 0.0)
        carry = jnp.exp(jnp.full((1, HEAD_DIM), -rate * rows, jnp.float32))
        carry = jnp.where(whole, carry, 0.0)
        incoming = near[n].astype(jnp.float32) + carry * far[n].astype(jnp.float32)
        cross = jnp.dot(
            queries[:, columns], incoming.astype(jnp.bfloat16), preferred_element_type=jnp.float32
        )
        attention = intra[:, columns] + cross * weight
        opened = jax.nn.sigmoid(gate[:, columns].astype(jnp.float32))
        out[:, columns] = (attention * gain[:, columns].astype(jnp.float32) * opened).astype(
            jnp.bfloat16
        )
        total[...] += attention * attention

    @pl.when(pl.program_id(0) == pl.num_programs(0) - 1)
    def _():
        squares[...] = lax.dot_general(
            jnp.ones((8, HEAD_DIM), jnp.float32),
            total[...],
            NT,
            precision=lax.Precision.HIGHEST,
            preferred_element_type=jnp.float32,
        )


def product_kernel(*refs, lefts, weights, tile, plan):
    out, stream, sems = refs[lefts + weights :]
    copies, place = [], 0
    for n in range(weights):
        weight = refs[lefts + n]
        for start in range(0, weight.shape[0], tile):
            copies.append(
                pltpu.make_async_copy(
                    weight.at[pl.ds(start, tile)], stream.at[pl.ds(place, tile)], sems.at[place // tile]
                )
            )
            place += tile
    for copy in copies:
        copy.start()
    for first, rows, left, row, column in plan:
        left = refs[left]
        for start in range(first, first + rows, tile):
            if left is refs[0]:
                copies[start // tile].wait()
            made = lax.dot_general(
                left[...], stream[pl.ds(start, tile)], NT, preferred_element_type=jnp.float32
            )
            out[pl.ds(row, left.shape[0]), pl.ds(column + start - first, tile)] = made.astype(
                jnp.bfloat16
            )


def end_kernel(own, other, own_turned, other_turned, weight, weight_turned, *outs):
    rows = own.shape[0]
    places = outs if len(outs) == 2 else [outs[0].at[pl.ds(n * rows, rows)] for n in range(2)]
    for one, two, out in zip((own, other), (own_turned, other_turned), places):
        total = lax.dot_general(one[...], weight[...], NT, preferred_element_type=jnp.float32)
        total += lax.dot_general(
            two[...], weight_turned[...], NT, preferred_element_type=jnp.float32
        )
        out[...] = total.astype(jnp.bfloat16)


def added(one, two):
    return (one.astype(jnp.float32) + two.astype(jnp.float32)).astype(jnp.bfloat16)


def split_kernel(where, made, come, kept, sent):
    half = kept.shape[1]
    keeps_low = (where[2] ^ (where[0] - 1)) & 2 == 0
    total = added(made[...], come[...])
    for value, first, second in ((True, kept, sent), (False, sent, kept)):

        @pl.when(keeps_low == value)
        def _(first=first, second=second):
            first[...] = total[:, :half]
            second[...] = total[:, half:]


def pair_kernel(where, own, own_come, two, two_come, kept, sent):
    keeps_own = (where[2] ^ where[0]) & 2 == 0
    for value, first, second in ((True, kept, sent), (False, sent, kept)):

        @pl.when(keeps_own == value)
        def _(first=first, second=second):
            first[...] = added(own[...], own_come[...])
            second[...] = added(two[...], two_come[...])


def add_kernel(*refs):
    out, column = refs[-1], 0
    for one, two in zip(refs[:-1:2], refs[1::2]):
        here = one.shape[1]
        out[:, column : column + here] = added(one[...], two[...])
        column += here


def run(sems, *pairs):
    copies = [pltpu.make_async_copy(a, b, sems.at[n]) for n, (a, b) in enumerate(pairs)]
    for copy in copies:
        copy.start()
    for copy in copies:
        copy.wait()


def cut_kernel(where, weight, low_a, low_b, high, sems):
    rows, first = high.shape[0], low_a.shape[0]
    start = where[1] * rows

    def part(at, ref):
        return weight.at[pl.ds(pl.multiple_of(start + at, 128), ref.shape[0])], ref

    run(sems, part(0, low_a), part(0, high), part(first, low_b))


def pick_kernel(where, low, high, *refs, upper, start):
    outs, sems = refs[:-1], refs[-1]
    for above, source, offset in ((True, low, 0), (False, high, start)):

        @pl.when((where[0] >= upper) == above)
        def _(source=source, offset=offset):
            pairs, at = [], offset
            for out in outs:
                pairs.append((source.at[pl.ds(at, out.shape[0])], out))
                at += out.shape[0]
            run(sems, *pairs)


def scale_of(squares, more, width):
    mean = jnp.transpose(squares[...] + more[...])[:, :1] / width
    return lax.rsqrt(mean + 1e-06)


def at_end(where, count):
    return ((where[0] == 0) | (where[0] == count - 1)) & (where[0] ^ where[2] == count - 1)


def most_kernel(
    where, squares, squares_more, kept_a, more_a, kept_b, more_b, back, near, near_more, near_back,
    end_a, end_a_more, end_b, end_b_more, end_back, out, one, two, sems, *, width, count
):
    rows, full = out.shape
    half = full // 2
    cut = end_a.shape[1]
    scale = scale_of(squares, squares_more, width)
    apart = where[0] ^ where[2]
    end = at_end(where, count)
    beside = (apart & 1 == 1) & ~end
    low, high = pl.ds(0, rows), pl.ds(rows, rows)
    first, second = pl.ds(0, cut), pl.ds(cut, cut)
    most, others = pl.ds(0, 2 * cut), pl.ds(2 * cut, half - 2 * cut)

    def put(start, *parts):
        total = sum(part.astype(jnp.float32) for part in parts)
        out[:, pl.ds(start, parts[0].shape[1])] = (total * scale).astype(jnp.bfloat16)

    @pl.when(apart == 0)
    def _():
        run(
            sems,
            (kept_a, one.at[:, most]),
            (more_a, two.at[:, most]),
            (kept_b, one.at[:, others]),
            (more_b, two.at[:, others]),
        )
        for side in range(2):
            span = pl.ds(side * rows, rows)
            put(side * half, one[span], two[span])

    @pl.when(apart == 2)
    def _():
        run(
            sems,
            (kept_a.at[low], one.at[low, most]),
            (more_a.at[low], two.at[low, most]),
            (kept_b.at[low], one.at[low, others]),
            (more_b.at[low], two.at[low, others]),
            (back, one.at[high]),
        )

    @pl.when(beside)
    def _():
        run(
            sems,
            (near.at[low], one.at[low]),
            (near_more.at[low], two.at[low]),
            (near_back, one.at[high]),
        )

    @pl.when(end)
    def _():
        run(
            sems,
            (end_a.at[low], one.at[low, first]),
            (end_b.at[low], one.at[low, second]),
            (end_a_more.at[low], two.at[low, first]),
            (end_b_more.at[low], two.at[low, second]),
            (end_back, one.at[high, most]),
        )

    for group in range(2):
        this = group * half

        @pl.when((apart > 0) & ~end & (where[1] == group))
        def _(this=this):
            put(this, one[low], two[low])
            put(half - this, one[high])

        @pl.when(end & (where[1] == group))
        def _(this=this):
            put(this, one[low, : 2 * cut], two[low, : 2 * cut])
            put(half - this, one[high, : 2 * cut])


def last_kernel(
    where, squares, squares_more, kept, more, across, back, most, out, this, that, sems, *, width, count
):
    half, cut = out.shape[1] // 2, kept.shape[1]
    for group in range(2):

        @pl.when(at_end(where, count) & (where[1] == group))
        def _(group=group):
            scale = scale_of(squares, squares_more, width)
            for to, one, two in ((this, kept, more), (that, across, back)):
                total = one[...].astype(jnp.float32) + two[...].astype(jnp.float32)
                to[...] = (total * scale).astype(jnp.bfloat16)
            pairs = [
                (ref, out.at[:, pl.ds(side * half + half - cut, cut)])
                for ref, side in ((this, group), (that, 1 - group))
            ]
            run(sems, *pairs)


def shards_grid(
    layer_queries,
    layer_keys,
    layer_values,
    gate_logits,
    norm_gain,
    decay_exponents,
    doc_lengths,
    out_weight,
):
    count, group, block, head = (
        lax.axis_size("seq"),
        lax.axis_index("groups"),
        lax.axis_index("seq"),
        lax.axis_index("head"),
    )
    tok_rows, wide = layer_queries.shape
    heads_here = decay_exponents.shape[0]
    half = out_weight.shape[0] // 2
    cut = half // 3
    span = tok_rows * count
    index = range(count)
    table = jax.ShapeDtypeStruct

    def across(value, pairs):
        return lax.ppermute(
            value, ("seq", "head"), [(b * count + h, b * count + k) for b, h, k in pairs]
        )

    where = jnp.stack([block, group, head])

    up = [(i, i + 1) for i in range(count - 1)]
    down = [(i + 1, i) for i in range(count - 1)]
    low_a, low_b, mine = pl.pallas_call(
        cut_kernel,
        in_specs=[SMEM, HBM],
        out_shape=[
            pltpu.VMEM((rows, wide), jnp.bfloat16) for rows in (2 * cut, cut, half)
        ],
        scratch_shapes=[pltpu.SemaphoreType.DMA((3,))],
        compiler_params=limit(2),
    )(where, out_weight)
    low = [lax.ppermute(low_a, "seq", up), lax.ppermute(low_b, "seq", up)]
    high = lax.ppermute(mine, "seq", down)
    low2 = [lax.ppermute(low[n], "seq", up[1:]) for n in range(2)]
    high2 = lax.ppermute(high, "seq", down[:-1])

    def pick(part, start, outs):
        return pl.pallas_call(
            functools.partial(pick_kernel, upper=count // 2, start=start),
            in_specs=[SMEM, HBM, HBM],
            out_shape=[pltpu.VMEM((cut, wide), jnp.bfloat16)] * outs,
            scratch_shapes=[pltpu.SemaphoreType.DMA((outs,))],
            compiler_params=limit(2),
        )(where, part, high2)

    far2 = [*pick(low2[0], 0, 2), *pick(low2[1], 2 * cut, 1)]
    ends = {0: (count - 1, 1), count - 1: (0, count - 2)}
    far3 = []
    for part in far2:
        same, cross = (
            lax.ppermute(
                part,
                ("seq", "head"),
                [
                    (b * count + (h ^ turn), end * count + h)
                    for end, (f, b) in ends.items()
                    for h in index
                    if (h ^ f) & 1 == 0
                ],
            )
            for turn in (0, 1)
        )
        far3.append((same, cross))
    ends = {end: f for end, (f, _) in ends.items()}

    columns = pl.BlockSpec((tok_rows, wide // STEPS), lambda n: (0, n))
    square = pl.BlockSpec((heads_here // STEPS, HEAD_DIM, HEAD_DIM), lambda n: (n, 0, 0))
    state = pl.pallas_call(
        functools.partial(state_kernel, span=span),
        grid=(STEPS,),
        in_specs=[SMEM, SMEM, SMEM, columns, columns],
        out_specs=square,
        out_shape=table((heads_here, HEAD_DIM, HEAD_DIM), jnp.bfloat16),
        compiler_params=limit(8),
    )(where, doc_lengths, decay_exponents, layer_keys, layer_values)
    near_state = lax.ppermute(state, "seq", up)
    far_state = lax.ppermute(state, "seq", [(i, i + 2) for i in range(count - 2)])
    intra = pl.pallas_call(
        functools.partial(intra_kernel, span=span),
        grid=(STEPS,),
        in_specs=[SMEM, SMEM, SMEM, columns, columns, columns],
        out_specs=columns,
        out_shape=table((tok_rows, wide), jnp.float32),
        compiler_params=limit(12),
    )(where, doc_lengths, decay_exponents, layer_queries, layer_keys, layer_values)
    gated, squares = pl.pallas_call(
        functools.partial(gate_kernel, span=span),
        grid=(STEPS,),
        in_specs=[
            SMEM, SMEM, SMEM, columns, columns, square, square,
            pl.BlockSpec((1, wide // STEPS), lambda n: (0, n)), columns,
        ],
        out_specs=[columns, pl.BlockSpec((8, tok_rows), lambda n: (0, 0))],
        out_shape=[table((tok_rows, wide), jnp.bfloat16), table((8, tok_rows), jnp.float32)],
        scratch_shapes=[pltpu.VMEM((tok_rows, HEAD_DIM), jnp.float32)],
        compiler_params=limit(12),
    )(
        where, doc_lengths, decay_exponents, layer_queries, intra, near_state, far_state,
        norm_gain[None, :], gate_logits,
    )
    other = lax.ppermute(gated, "groups", [(0, 1), (1, 0)])
    turned = [
        across(value, [(b, h, h ^ 1) for b in index for h in index])
        for value in (gated, other)
    ]
    squares = squares + lax.ppermute(squares, "head", [(i, i ^ 1) for i in index])
    squares_more = lax.ppermute(squares, "head", [(i, i ^ 2) for i in index])

    def product(shape, lefts, weights, plan, space=ANY):
        total = sum(weight.shape[0] for weight in weights)
        tile = 256
        return pl.pallas_call(
            functools.partial(
                product_kernel, lefts=len(lefts), weights=len(weights), tile=tile, plan=plan
            ),
            in_specs=[pl.BlockSpec()] * len(lefts) + [space] * len(weights),
            out_shape=pltpu.VMEM(shape, jnp.bfloat16),
            scratch_shapes=[
                pltpu.VMEM((total, wide), jnp.bfloat16),
                pltpu.SemaphoreType.DMA((total // tile,)),
            ],
            compiler_params=limit(12),
            cost_estimate=cost(2 * shape[0] * shape[1] * wide, 8),
        )(*lefts, *weights)

    def for_both(*weights):
        plan, column = [], 0
        for weight in weights:
            rows = weight.shape[0]
            plan += [(column, rows, side, side * tok_rows, column) for side in range(2)]
            column += rows
        return product((2 * tok_rows, column), (gated, other), weights, plan)

    def split(made, come):
        rows = 2 * tok_rows // STEPS
        return pl.pallas_call(
            split_kernel,
            grid=(STEPS,),
            in_specs=[SMEM] + [pl.BlockSpec((rows, 2 * half), lambda n: (n, 0))] * 2,
            out_specs=[pl.BlockSpec((rows, half), lambda n: (n, 0))] * 2,
            out_shape=[pltpu.VMEM((2 * tok_rows, half), jnp.bfloat16)] * 2,
            compiler_params=limit(8),
            cost_estimate=cost(4 * tok_rows * half, 9),
        )(where, made, come)

    def pair(own, two, start):
        rows, width = two[0].shape
        size = (rows // 2, cut)
        shifted = pl.BlockSpec(size, lambda n, c: (n, c + start // cut))
        plain = pl.BlockSpec(size, lambda n, c: (n, c))
        return pl.pallas_call(
            pair_kernel,
            grid=(2, width // cut),
            in_specs=[SMEM, shifted, shifted, plain, plain],
            out_specs=[plain, plain],
            out_shape=[pltpu.VMEM((rows, width), jnp.bfloat16)] * 2,
            compiler_params=limit(8),
            cost_estimate=cost(rows * width, 6),
        )(where, *own, *two)

    def add(*pairs, part=0, parts=1):
        rows, width = pairs[0][0].shape[0] // parts, sum(one.shape[1] for one, _ in pairs)
        steps = 2
        operands = [value for pair in pairs for value in pair]

        def block(width, part=0):
            return pl.BlockSpec((rows // steps, width), lambda n: (part * steps + n, 0))

        return pl.pallas_call(
            add_kernel,
            grid=(steps,),
            in_specs=[block(value.shape[1], part) for value in operands],
            out_specs=block(width),
            out_shape=pltpu.VMEM((rows, width), jnp.bfloat16),
            compiler_params=limit(6),
            cost_estimate=cost(rows * width, 3),
        )(*operands)

    def from_core(made, wanted):
        pairs = [(b, h, h ^ 1) for b, f in wanted.items() for h in index if (h ^ f) & 1]
        return across(made, pairs)

    def anywhere(value, pairs):
        flat = [tuple((g * count + b) * count + h for g, b, h in pair) for pair in pairs]
        return lax.ppermute(value, ("groups", "seq", "head"), flat)

    def give_back(total, owners):
        return anywhere(total, [((g, b, f), (1 - g, b, f)) for g in range(2) for b, f in owners])

    plan = [(side * half, half, 0, side * tok_rows, 0) for side in range(2)]
    made = product((2 * tok_rows, half), (gated,), (out_weight,), plan, HBM)
    own = (made, from_core(made, {b: b for b in index}))

    nears = [(b, f) for b in index for f in (b - 1, b + 1) if 0 <= f < count]
    made = for_both(*low, high)
    come = from_core(made, {b: f for b, f in nears})
    near_kept, near_sent = split(made, come)
    near_more = across(near_sent, [(b, f ^ 2, f) for b, f in nears])
    near_back = give_back(add((near_kept, near_more), part=1, parts=2), nears)

    pieces = []
    for n, part in enumerate((far2[:2], far2[2:])):
        made = for_both(*part)
        two = (made, from_core(made, {b: b ^ 2 for b in index}))
        kept, sent = pair(own, two, 2 * n * cut)
        more = across(sent, [(b, h, h ^ 2) for b in index for h in (b, b ^ 2)])
        pieces.append((kept, more))
    back = give_back(add(*pieces, part=1, parts=2), [(b, b ^ 2) for b in index])

    last = []
    for n, part in enumerate(far3):
        parts = 1 if n < 2 else 2
        made = pl.pallas_call(
            end_kernel,
            out_shape=[pltpu.VMEM((2 * tok_rows // parts, cut), jnp.bfloat16)] * parts,
            compiler_params=limit(12),
            cost_estimate=cost(8 * tok_rows * cut * wide, 8),
        )(gated, other, *turned, *part)
        last.append((made[0], across(made[0], [(b, f ^ 2, f) for b, f in ends.items()])))
    first_back = give_back(add(*last[:2], part=1, parts=2), ends.items())
    pairs = [((g, b, f ^ 2), (1 - g, b, f)) for g in range(2) for b, f in ends.items()]
    last_back = anywhere(made[1], pairs), give_back(made[1], ends.items())

    sizes = {"width": wide * count, "count": count}
    most = pl.pallas_call(
        functools.partial(most_kernel, **sizes),
        in_specs=[SMEM, pl.BlockSpec(), pl.BlockSpec()] + [ANY] * 13,
        out_shape=table((tok_rows, 2 * half), jnp.bfloat16),
        scratch_shapes=[
            pltpu.VMEM((2 * tok_rows, half), jnp.bfloat16),
            pltpu.VMEM((2 * tok_rows, half), jnp.bfloat16),
            pltpu.SemaphoreType.DMA((6,)),
        ],
        compiler_params=limit(8),
    )(
        where, squares, squares_more, *pieces[0], *pieces[1], back,
        near_kept, near_more, near_back, *last[0], *last[1], first_back,
    )
    return pl.pallas_call(
        functools.partial(last_kernel, **sizes),
        in_specs=[SMEM] + [pl.BlockSpec()] * 6 + [HBM],
        out_specs=HBM,
        out_shape=table((tok_rows, 2 * half), jnp.bfloat16),
        scratch_shapes=[
            pltpu.VMEM((tok_rows, cut), jnp.bfloat16),
            pltpu.VMEM((tok_rows, cut), jnp.bfloat16),
            pltpu.SemaphoreType.DMA((2,)),
        ],
        input_output_aliases={7: 0},
        compiler_params=limit(4),
    )(where, squares, squares_more, *last[2], *last_back, most)


def shards_general(
    layer_queries,
    layer_keys,
    layer_values,
    gate_logits,
    norm_gain,
    decay_exponents,
    doc_lengths,
    out_weight,
):
    tok_rows = layer_queries.shape[0]
    decay_rate, block_state, intra, cross = attention_parts(
        layer_queries, layer_keys, layer_values, decay_exponents, doc_lengths
    )
    count, block = lax.axis_size("seq"), lax.axis_index("seq")
    states = lax.all_gather(block_state, "seq")

    def turn(position, running):
        carry = carry_of(position, decay_rate, doc_lengths, tok_rows)
        longer = carry[:, None, None] * running + states[position]
        return jnp.where(position < block, longer, running)

    incoming = lax.fori_loop(0, count - 1, turn, jnp.zeros_like(block_state))
    attention = (intra() + cross(incoming)).reshape(layer_queries.shape)
    squares = lax.psum(jnp.sum(attention * attention, axis=1), "head")
    width_all = layer_queries.shape[1] * lax.axis_size("head")
    inv_scale = lax.rsqrt(squares / width_all + 1e-06)
    gated_out = (
        attention
        * inv_scale[:, None]
        * norm_gain.astype(jnp.float32)
        * jax.nn.sigmoid(gate_logits.astype(jnp.float32))
    ).astype(jnp.bfloat16)
    partials = lax.dot_general(
        gated_out,
        lax.all_gather(out_weight, "seq", axis=0, tiled=True),
        NT,
        preferred_element_type=jnp.float32,
    )
    return lax.psum_scatter(partials, "head", scatter_dimension=1, tiled=True).astype(jnp.bfloat16)


def solution(mesh):
    in_specs = (
        P(("groups", "seq"), "head"),
        P(("groups", "seq"), "head"),
        P(("groups", "seq"), "head"),
        P(("groups", "seq"), "head"),
        P("head"),
        P("head"),
        P("groups"),
        P("seq", "head"),
    )
    out_specs = P(("groups", "seq"), "head")
    seq, head = mesh.shape["seq"], mesh.shape["head"]
    grid = seq == head == 4 and mesh.shape["groups"] == 2
    shards = shards_grid if grid else shards_general
    return jax.shard_map(shards, mesh=mesh, in_specs=in_specs, out_specs=out_specs, check_vma=False)
```

profile of v0, /device:TPU:14, one launch (start us, length us, event | category | flops | bytes accessed | tf_op | source)
XLA Modules:
  0.0 186.9 jit_solution(6863739875568675954)
XLA Ops:
  0.1 1.9 %copy-done.3 = bf16[1536,1024]{1,0:T(8,128)(2,1)S(1)} copy-done((bf16[1536,1024]{1,0:T(8,128)(2,1)S(1)}, bf16[1536,1024]{1,0:T(8,128)(2,1)}, u32[]{:S(2)}) %copy-start.3) | copy-done | bytes 3145752
  2.8 2.5 %collective-permute-start.9 = (bf16[768,1024]{1,0:T(8,128)(2,1)S(1)}, bf16[768,1024]{1,0:T(8,128)(2,1)S(1)}, u32[]{:S(2)}, u32[]{:S(2)}) collective-permute-start(bf16[768,1024]{1,0:T(8,128)(2,1)S(1)} %get-tuple-element.23), channel_id=1, source_target_pairs={{4,0},{8,4},{12,8},{5,1},{9,5},{13,9},{6,2},{10,6},{14,10},{7,3},{... | collective-permute-start | bytes 4718600 | tf_op jit(solution)/shard_map/ppermute | solution.py:453
  5.3 2.4 %shard_map.83 = bf16[8,128,128]{2,1,0:T(8,128)(2,1)S(1)} custom-call(s32[3]{0:T(128)S(1)} %pad_add_fusion.where, s32[4]{0:T(128)S(1)} %copy-done.6, s32[8]{0:T(128)S(1)} %copy-done.7, bf16[512,1024]{1,0:T(8,128)(2,1)S(1)} %copy-done, bf16[512,1024]{1,0:T(8,128)(2,1)S(1)} %copy-done.1), custom_call_target="tpu_custom_call" | custom-call | tf_op jit(solution)/shard_map/pallas_call | solution.py:488
  7.8 4.6 %collective-permute-start.1 = (bf16[8,128,128]{2,1,0:T(8,128)(2,1)S(1)}, bf16[8,128,128]{2,1,0:T(8,128)(2,1)S(1)}, u32[]{:S(2)}, u32[]{:S(2)}) collective-permute-start(bf16[8,128,128]{2,1,0:T(8,128)(2,1)S(1)} %shard_map.83), channel_id=1, source_target_pairs={{0,8},{4,12},{1,9},{5,13},{2,10},{6,14},{3,11},{7,15},{16,24},{20,... | collective-permute-start | bytes 786440 | tf_op jit(solution)/shard_map/ppermute | solution.py:497
  12.4 1.9 %collective-permute-start = (bf16[8,128,128]{2,1,0:T(8,128)(2,1)S(1)}, bf16[8,128,128]{2,1,0:T(8,128)(2,1)S(1)}, u32[]{:S(2)}, u32[]{:S(2)}) collective-permute-start(bf16[8,128,128]{2,1,0:T(8,128)(2,1)S(1)} %shard_map.83), channel_id=1, source_target_pairs={{0,4},{4,8},{8,12},{1,5},{5,9},{9,13},{2,6},{6,10},{10,14},{3,7},{... | collective-permute-start | bytes 786440 | tf_op jit(solution)/shard_map/ppermute | solution.py:496
  14.3 1.9 %collective-permute-start.17 = (bf16[512,1024]{1,0:T(8,128)(2,1)S(1)}, bf16[512,1024]{1,0:T(8,128)(2,1)S(1)}, u32[]{:S(2)}, u32[]{:S(2)}) collective-permute-start(bf16[512,1024]{1,0:T(8,128)(2,1)S(1)} %get-tuple-element.26), channel_id=1, source_target_pairs={{0,4},{4,8},{8,12},{1,5},{5,9},{9,13},{2,6},{6,10},{10,14},{3,7},{... | collective-permute-start | bytes 3145736 | tf_op jit(solution)/shard_map/ppermute | solution.py:452
  16.3 5.1 %shard_map.82.intra = f32[512,1024]{1,0:T(8,128)S(1)} custom-call(s32[3]{0:T(128)S(1)} %pad_add_fusion.where, s32[4]{0:T(128)S(1)} %copy-done.6, s32[8]{0:T(128)S(1)} %copy-done.7, bf16[512,1024]{1,0:T(8,128)(2,1)S(1)} %copy-done.2, bf16[512,1024]{1,0:T(8,128)(2,1)S(1)} %copy-done, bf16[512,1024]{1,0:T(8,128)(2,1)S(1)} %copy-done.1), custom_call_target="tpu_custom_call" | custom-call | tf_op jit(solution)/shard_map/pallas_call | solution.py:498
  21.4 1.8 collective-permute-done.1.far
  23.2 5.6 %collective-permute-done.near = bf16[8,128,128]{2,1,0:T(8,128)(2,1)S(1)} collective-permute-done((bf16[8,128,128]{2,1,0:T(8,128)(2,1)S(1)}, bf16[8,128,128]{2,1,0:T(8,128)(2,1)S(1)}, u32[]{:S(2)}, u32[]{:S(2)}) %collective-permute-start) | collective-permute-done | bytes 262176 | tf_op jit(solution)/shard_map/ppermute | solution.py:496
  28.8 3.6 %shard_map.84 = (bf16[512,1024]{1,0:T(8,128)(2,1)S(1)}, f32[8,512]{1,0:T(8,128)S(1)}) custom-call(s32[3]{0:T(128)S(1)} %pad_add_fusion.where, s32[4]{0:T(128)S(1)} %copy-done.6, s32[8]{0:T(128)S(1)} %copy-done.7, bf16[512,1024]{1,0:T(8,128)(2,1)S(1)} %copy-done.2, f32[512,1024]{1,0:T(8,128)S(1)} %shard_map.82.intra, ...), custom_call_target="tpu_custom_call" | custom-call | tf_op jit(solution)/shard_map/pallas_call | solution.py:506
  33.0 4.6 %collective-permute-start.7 = (bf16[256,1024]{1,0:T(8,128)(2,1)S(1)}, bf16[256,1024]{1,0:T(8,128)(2,1)S(1)}, u32[]{:S(2)}, u32[]{:S(2)}) collective-permute-start(bf16[256,1024]{1,0:T(8,128)(2,1)S(1)} %get-tuple-element.22), channel_id=1, source_target_pairs={{0,4},{4,8},{8,12},{1,5},{5,9},{9,13},{2,6},{6,10},{10,14},{3,7},{... | collective-permute-start | bytes 1572872 | tf_op jit(solution)/shard_map/ppermute | solution.py:452
  37.6 24.8 %collective-permute-done.7.refs_3_ = bf16[256,1024]{1,0:T(8,128)(2,1)S(1)} collective-permute-done((bf16[256,1024]{1,0:T(8,128)(2,1)S(1)}, bf16[256,1024]{1,0:T(8,128)(2,1)S(1)}, u32[]{:S(2)}, u32[]{:S(2)}) %collective-permute-start.7) | collective-permute-done | bytes 524320 | tf_op jit(solution)/shard_map/ppermute | solution.py:452
  62.4 5.8 %shard_map.95.made = bf16[1024,1536]{1,0:T(8,128)(2,1)S(1)} custom-call(bf16[512,1024]{1,0:T(8,128)(2,1)S(1)} %get-tuple-element.21.own.refs_0_, bf16[512,1024]{1,0:T(8,128)(2,1)S(1)} %collective-permute-done.4.other.refs_1_, bf16[512,1024]{1,0:T(8,128)(2,1)S(1)} %collective-permute-done.17.refs_2_, bf16[256,1024]{1,0:T(8,128)(2,1)S(1)} %collective-permute-done.7.refs_3_, ...), custom_call_target="tpu_custom_call" | custom-call | flops 3221225472 | bytes 8388608 | tf_op jit(solution)/shard_map/pallas_call | solution.py:532
  69.5 1.9 %collective-permute-start.10 = (bf16[768,1024]{1,0:T(8,128)(2,1)S(1)}, bf16[768,1024]{1,0:T(8,128)(2,1)S(1)}, u32[]{:S(2)}, u32[]{:S(2)}) collective-permute-start(bf16[768,1024]{1,0:T(8,128)(2,1)S(1)} %collective-permute-done.9.refs_4_), channel_id=1, source_target_pairs={{4,0},{8,4},{5,1},{9,5},{6,2},{10,6},{7,3},{11,7},{20,16},{24,20},... | collective-permute-start | bytes 4718600 | tf_op jit(solution)/shard_map/ppermute | solution.py:455
  71.4 4.8 %collective-permute-start.18 = (bf16[512,1024]{1,0:T(8,128)(2,1)S(1)}, bf16[512,1024]{1,0:T(8,128)(2,1)S(1)}, u32[]{:S(2)}, u32[]{:S(2)}) collective-permute-start(bf16[512,1024]{1,0:T(8,128)(2,1)S(1)} %collective-permute-done.17.refs_2_), channel_id=1, source_target_pairs={{4,8},{8,12},{5,9},{9,13},{6,10},{10,14},{7,11},{11,15},{20,24},{2... | collective-permute-start | bytes 3145736 | tf_op jit(solution)/shard_map/ppermute | solution.py:454
  76.2 4.6 %shard_map.88.own = bf16[1024,768]{1,0:T(8,128)(2,1)S(1)} custom-call(bf16[512,1024]{1,0:T(8,128)(2,1)S(1)} %get-tuple-element.21.own.refs_0_, bf16[1536,1024]{1,0:T(8,128)(2,1)S(1)} %copy-done.4), custom_call_target="tpu_custom_call" | custom-call | flops 1610612736 | bytes 8388608 | tf_op jit(solution)/shard_map/pallas_call | solution.py:532
  80.8 2.1 %collective-permute-start.16 = (bf16[1024,768]{1,0:T(8,128)(2,1)S(1)}, bf16[1024,768]{1,0:T(8,128)(2,1)S(1)}, u32[]{:S(2)}, u32[]{:S(2)}) collective-permute-start(bf16[1024,768]{1,0:T(8,128)(2,1)S(1)} %shard_map.88.own), channel_id=1, source_target_pairs={{1,0},{3,2},{4,5},{6,7},{9,8},{11,10},{12,13},{14,15},{17,16},{19,... | collective-permute-start | bytes 4718600 | tf_op jit(solution)/shard_map/ppermute | solution.py:435
  84.3 15.4 %collective-permute-done.18.low = bf16[512,1024]{1,0:T(8,128)(2,1)S(1)} collective-permute-done((bf16[512,1024]{1,0:T(8,128)(2,1)S(1)}, bf16[512,1024]{1,0:T(8,128)(2,1)S(1)}, u32[]{:S(2)}, u32[]{:S(2)}) %collective-permute-start.18) | collective-permute-done | bytes 1048608 | tf_op jit(solution)/shard_map/ppermute | solution.py:454
  99.7 9.4 %collective-permute-done.10.high = bf16[768,1024]{1,0:T(8,128)(2,1)S(1)} collective-permute-done((bf16[768,1024]{1,0:T(8,128)(2,1)S(1)}, bf16[768,1024]{1,0:T(8,128)(2,1)S(1)}, u32[]{:S(2)}, u32[]{:S(2)}) %collective-permute-start.10) | collective-permute-done | bytes 1572896 | tf_op jit(solution)/shard_map/ppermute | solution.py:455
  111.3 1.9 %collective-permute-start.19 = (bf16[1024,512]{1,0:T(8,128)(2,1)S(1)}, bf16[1024,512]{1,0:T(8,128)(2,1)S(1)}, u32[]{:S(2)}, u32[]{:S(2)}) collective-permute-start(bf16[1024,512]{1,0:T(8,128)(2,1)S(1)} %shard_map.90.two), channel_id=1, source_target_pairs={{1,0},{3,2},{4,5},{6,7},{9,8},{11,10},{12,13},{14,15},{17,16},{19,... | collective-permute-start | bytes 3145736 | tf_op jit(solution)/shard_map/ppermute | solution.py:435
  114.7 2.4 %collective-permute-start.21 = (bf16[1024,256]{1,0:T(8,128)(2,1)S(1)}, bf16[1024,256]{1,0:T(8,128)(2,1)S(1)}, u32[]{:S(2)}, u32[]{:S(2)}) collective-permute-start(bf16[1024,256]{1,0:T(8,128)(2,1)S(1)} %shard_map.92.two), channel_id=1, source_target_pairs={{1,0},{3,2},{4,5},{6,7},{9,8},{11,10},{12,13},{14,15},{17,16},{19,... | collective-permute-start | bytes 1572872 | tf_op jit(solution)/shard_map/ppermute | solution.py:435
  118.5 2.2 %shard_map.96 = (bf16[1024,768]{1,0:T(8,128)(2,1)S(1)}, bf16[1024,768]{1,0:T(8,128)(2,1)S(1)}) custom-call(s32[3]{0:T(128)S(1)} %pad_add_fusion.where, bf16[1024,1536]{1,0:T(8,128)(2,1)S(1)} %shard_map.95.made, bf16[1024,1536]{1,0:T(8,128)(2,1)S(1)} %collective-permute-done.24.come), custom_call_target="tpu_custom_call" | custom-call | flops 1572864 | bytes 9437184 | tf_op jit(solution)/shard_map/pallas_call | solution.py:556
  120.8 2.4 %collective-permute-start.25 = (bf16[1024,768]{1,0:T(8,128)(2,1)S(1)}, bf16[1024,768]{1,0:T(8,128)(2,1)S(1)}, u32[]{:S(2)}, u32[]{:S(2)}) collective-permute-start(bf16[1024,768]{1,0:T(8,128)(2,1)S(1)} %get-tuple-element.34), channel_id=1, source_target_pairs={{3,1},{6,4},{4,6},{11,9},{9,11},{12,14},{19,17},{22,20},{20,22},{2... | collective-permute-start | bytes 4718600 | tf_op jit(solution)/shard_map/ppermute | solution.py:435
  123.9 1.6 shard_map.91
  125.6 1.7 collective-permute-start.31
  131.6 7.9 %collective-permute-done.31.weight_turned = bf16[256,1024]{1,0:T(8,128)(2,1)S(1)} collective-permute-done((bf16[256,1024]{1,0:T(8,128)(2,1)S(1)}, bf16[256,1024]{1,0:T(8,128)(2,1)S(1)}, u32[]{:S(2)}, u32[]{:S(2)}) %collective-permute-start.31) | collective-permute-done | bytes 524320 | tf_op jit(solution)/shard_map/ppermute | solution.py:471
  142.2 6.6 %collective-permute-start.12 = (bf16[256,1024]{1,0:T(8,128)(2,1)S(1)}, bf16[256,1024]{1,0:T(8,128)(2,1)S(1)}, u32[]{:S(2)}, u32[]{:S(2)}) collective-permute-start(bf16[256,1024]{1,0:T(8,128)(2,1)S(1)} %shard_map.86.refs_2_), channel_id=1, source_target_pairs={{4,1},{6,3},{9,12},{11,14},{20,17},{22,19},{25,28},{27,30}} | collective-permute-start | bytes 1572872 | tf_op jit(solution)/shard_map/ppermute | solution.py:471
  149.5 5.4 %collective-permute-done.25.refs_1_.near_more = bf16[1024,768]{1,0:T(8,128)(2,1)S(1)} collective-permute-done((bf16[1024,768]{1,0:T(8,128)(2,1)S(1)}, bf16[1024,768]{1,0:T(8,128)(2,1)S(1)}, u32[]{:S(2)}, u32[]{:S(2)}) %collective-permute-start.25) | collective-permute-done | bytes 1572896 | tf_op jit(solution)/shard_map/ppermute | solution.py:435
  154.9 7.0 %collective-permute-start.2 = (f32[8,512]{1,0:T(8,128)S(1)}, f32[8,512]{1,0:T(8,128)S(1)}, u32[]{:S(2)}, u32[]{:S(2)}) collective-permute-start(f32[8,512]{1,0:T(8,128)S(1)} %get-tuple-element.20), channel_id=1, source_target_pairs={{0,1},{1,0},{2,3},{3,2},{4,5},{5,4},{6,7},{7,6},{8,9},{9,8},{10,11... | collective-permute-start | bytes 49160 | tf_op jit(solution)/shard_map/ppermute | solution.py:526
  163.0 2.4 %collective-permute-start.26 = (bf16[512,768]{1,0:T(8,128)(2,1)S(1)}, bf16[512,768]{1,0:T(8,128)(2,1)S(1)}, u32[]{:S(2)}, u32[]{:S(2)}) collective-permute-start(bf16[512,768]{1,0:T(8,128)(2,1)S(1)} %shard_map.97), channel_id=1, source_target_pairs={{1,17},{4,20},{6,22},{9,25},{11,27},{14,30},{17,1},{20,4},{22,6},{... | collective-permute-start | bytes 2359304 | tf_op jit(solution)/shard_map/ppermute | solution.py:605
  171.6 12.1 %collective-permute-done.26.near_back = bf16[512,768]{1,0:T(8,128)(2,1)S(1)} collective-permute-done((bf16[512,768]{1,0:T(8,128)(2,1)S(1)}, bf16[512,768]{1,0:T(8,128)(2,1)S(1)}, u32[]{:S(2)}, u32[]{:S(2)}) %collective-permute-start.26) | collective-permute-done | bytes 786464 | tf_op jit(solution)/shard_map/ppermute | solution.py:605
  183.7 2.4 %shard_map.101.most = bf16[512,1536]{1,0:T(8,128)(2,1)} custom-call(s32[3]{0:T(128)S(1)} %pad_add_fusion.where, f32[8,512]{1,0:T(8,128)S(1)} %add.3.squares, f32[8,512]{1,0:T(8,128)S(1)} %collective-permute-done.3.squares_more, bf16[1024,512]{1,0:T(8,128)(2,1)S(1)} %get-tuple-element.29.refs_0_.kept_a, ...), custom_call_target="tpu_custom_call" | custom-call | tf_op jit(solution)/shard_map/pallas_call | solution.py:645
  (78 shorter events, 25.3 us)
Async XLA Ops:
  2.8 59.6 %collective-permute-start.9 = (bf16[768,1024]{1,0:T(8,128)(2,1)S(1)}, bf16[768,1024]{1,0:T(8,128)(2,1)S(1)}, u32[]{:S(2)}, u32[]{:S(2)}) collective-permute-start(bf16[768,1024]{1,0:T(8,128)(2,1)S(1)} %get-tuple-element.23), channel_id=1, source_target_pairs={{4,0},{8,4},{12,8},{5,1},{9,5},{13,9},{6,2},{10,6},{14,10},{7,3},{... | collective-permute-start | bytes 4718600 | tf_op jit(solution)/shard_map/ppermute | solution.py:453
  7.8 15.4 %collective-permute-start.1 = (bf16[8,128,128]{2,1,0:T(8,128)(2,1)S(1)}, bf16[8,128,128]{2,1,0:T(8,128)(2,1)S(1)}, u32[]{:S(2)}, u32[]{:S(2)}) collective-permute-start(bf16[8,128,128]{2,1,0:T(8,128)(2,1)S(1)} %shard_map.83), channel_id=1, source_target_pairs={{0,8},{4,12},{1,9},{5,13},{2,10},{6,14},{3,11},{7,15},{16,24},{20,... | collective-permute-start | bytes 786440 | tf_op jit(solution)/shard_map/ppermute | solution.py:497
  12.4 16.4 %collective-permute-start = (bf16[8,128,128]{2,1,0:T(8,128)(2,1)S(1)}, bf16[8,128,128]{2,1,0:T(8,128)(2,1)S(1)}, u32[]{:S(2)}, u32[]{:S(2)}) collective-permute-start(bf16[8,128,128]{2,1,0:T(8,128)(2,1)S(1)} %shard_map.83), channel_id=1, source_target_pairs={{0,4},{4,8},{8,12},{1,5},{5,9},{9,13},{2,6},{6,10},{10,14},{3,7},{... | collective-permute-start | bytes 786440 | tf_op jit(solution)/shard_map/ppermute | solution.py:496
  14.3 48.1 %collective-permute-start.17 = (bf16[512,1024]{1,0:T(8,128)(2,1)S(1)}, bf16[512,1024]{1,0:T(8,128)(2,1)S(1)}, u32[]{:S(2)}, u32[]{:S(2)}) collective-permute-start(bf16[512,1024]{1,0:T(8,128)(2,1)S(1)} %get-tuple-element.26), channel_id=1, source_target_pairs={{0,4},{4,8},{8,12},{1,5},{5,9},{9,13},{2,6},{6,10},{10,14},{3,7},{... | collective-permute-start | bytes 3145736 | tf_op jit(solution)/shard_map/ppermute | solution.py:452
  32.4 30.1 %collective-permute-start.4 = (bf16[512,1024]{1,0:T(8,128)(2,1)S(1)}, bf16[512,1024]{1,0:T(8,128)(2,1)S(1)}, u32[]{:S(2)}, u32[]{:S(2)}) collective-permute-start(bf16[512,1024]{1,0:T(8,128)(2,1)S(1)} %get-tuple-element.21.own.refs_0_), channel_id=1, source_target_pairs={{0,16},{16,0},{1,17},{17,1},{2,18},{18,2},{3,19},{19,3},{4,20},{20... | collective-permute-start | bytes 3145736 | tf_op jit(solution)/shard_map/ppermute | solution.py:521
  33.0 29.5 %collective-permute-start.7 = (bf16[256,1024]{1,0:T(8,128)(2,1)S(1)}, bf16[256,1024]{1,0:T(8,128)(2,1)S(1)}, u32[]{:S(2)}, u32[]{:S(2)}) collective-permute-start(bf16[256,1024]{1,0:T(8,128)(2,1)S(1)} %get-tuple-element.22), channel_id=1, source_target_pairs={{0,4},{4,8},{8,12},{1,5},{5,9},{9,13},{2,6},{6,10},{10,14},{3,7},{... | collective-permute-start | bytes 1572872 | tf_op jit(solution)/shard_map/ppermute | solution.py:452
  68.2 49.0 %collective-permute-start.24 = (bf16[1024,1536]{1,0:T(8,128)(2,1)S(1)}, bf16[1024,1536]{1,0:T(8,128)(2,1)S(1)}, u32[]{:S(2)}, u32[]{:S(2)}) collective-permute-start(bf16[1024,1536]{1,0:T(8,128)(2,1)S(1)} %shard_map.95.made), channel_id=1, source_target_pairs={{0,1},{2,3},{5,4},{7,6},{8,9},{10,11},{13,12},{15,14},{16,17},{18,... | collective-permute-start | bytes 9437192 | tf_op jit(solution)/shard_map/ppermute | solution.py:435
  69.5 39.5 %collective-permute-start.10 = (bf16[768,1024]{1,0:T(8,128)(2,1)S(1)}, bf16[768,1024]{1,0:T(8,128)(2,1)S(1)}, u32[]{:S(2)}, u32[]{:S(2)}) collective-permute-start(bf16[768,1024]{1,0:T(8,128)(2,1)S(1)} %collective-permute-done.9.refs_4_), channel_id=1, source_target_pairs={{4,0},{8,4},{5,1},{9,5},{6,2},{10,6},{7,3},{11,7},{20,16},{24,20},... | collective-permute-start | bytes 4718600 | tf_op jit(solution)/shard_map/ppermute | solution.py:455
  71.4 28.2 %collective-permute-start.18 = (bf16[512,1024]{1,0:T(8,128)(2,1)S(1)}, bf16[512,1024]{1,0:T(8,128)(2,1)S(1)}, u32[]{:S(2)}, u32[]{:S(2)}) collective-permute-start(bf16[512,1024]{1,0:T(8,128)(2,1)S(1)} %collective-permute-done.17.refs_2_), channel_id=1, source_target_pairs={{4,8},{8,12},{5,9},{9,13},{6,10},{10,14},{7,11},{11,15},{20,24},{2... | collective-permute-start | bytes 3145736 | tf_op jit(solution)/shard_map/ppermute | solution.py:454
  80.8 39.9 %collective-permute-start.16 = (bf16[1024,768]{1,0:T(8,128)(2,1)S(1)}, bf16[1024,768]{1,0:T(8,128)(2,1)S(1)}, u32[]{:S(2)}, u32[]{:S(2)}) collective-permute-start(bf16[1024,768]{1,0:T(8,128)(2,1)S(1)} %shard_map.88.own), channel_id=1, source_target_pairs={{1,0},{3,2},{4,5},{6,7},{9,8},{11,10},{12,13},{14,15},{17,16},{19,... | collective-permute-start | bytes 4718600 | tf_op jit(solution)/shard_map/ppermute | solution.py:435
  82.9 30.3 %collective-permute-start.8 = (bf16[256,1024]{1,0:T(8,128)(2,1)S(1)}, bf16[256,1024]{1,0:T(8,128)(2,1)S(1)}, u32[]{:S(2)}, u32[]{:S(2)}) collective-permute-start(bf16[256,1024]{1,0:T(8,128)(2,1)S(1)} %collective-permute-done.7.refs_3_), channel_id=1, source_target_pairs={{4,8},{8,12},{5,9},{9,13},{6,10},{10,14},{7,11},{11,15},{20,24},{2... | collective-permute-start | bytes 1572872 | tf_op jit(solution)/shard_map/ppermute | solution.py:454
  99.7 15.1 %collective-permute-start.5 = (bf16[512,1024]{1,0:T(8,128)(2,1)S(1)}, bf16[512,1024]{1,0:T(8,128)(2,1)S(1)}, u32[]{:S(2)}, u32[]{:S(2)}) collective-permute-start(bf16[512,1024]{1,0:T(8,128)(2,1)S(1)} %get-tuple-element.21.own.refs_0_), channel_id=1, source_target_pairs={{0,1},{1,0},{2,3},{3,2},{4,5},{5,4},{6,7},{7,6},{8,9},{9,8},{10,11... | collective-permute-start | bytes 3145736 | tf_op jit(solution)/shard_map/ppermute | solution.py:435
  111.3 11.9 %collective-permute-start.19 = (bf16[1024,512]{1,0:T(8,128)(2,1)S(1)}, bf16[1024,512]{1,0:T(8,128)(2,1)S(1)}, u32[]{:S(2)}, u32[]{:S(2)}) collective-permute-start(bf16[1024,512]{1,0:T(8,128)(2,1)S(1)} %shard_map.90.two), channel_id=1, source_target_pairs={{1,0},{3,2},{4,5},{6,7},{9,8},{11,10},{12,13},{14,15},{17,16},{19,... | collective-permute-start | bytes 3145736 | tf_op jit(solution)/shard_map/ppermute | solution.py:435
  113.2 12.3 %collective-permute-start.6 = (bf16[512,1024]{1,0:T(8,128)(2,1)S(1)}, bf16[512,1024]{1,0:T(8,128)(2,1)S(1)}, u32[]{:S(2)}, u32[]{:S(2)}) collective-permute-start(bf16[512,1024]{1,0:T(8,128)(2,1)S(1)} %collective-permute-done.4.other.refs_1_), channel_id=1, source_target_pairs={{0,1},{1,0},{2,3},{3,2},{4,5},{5,4},{6,7},{7,6},{8,9},{9,8},{10,11... | collective-permute-start | bytes 3145736 | tf_op jit(solution)/shard_map/ppermute | solution.py:435
  114.7 12.5 %collective-permute-start.21 = (bf16[1024,256]{1,0:T(8,128)(2,1)S(1)}, bf16[1024,256]{1,0:T(8,128)(2,1)S(1)}, u32[]{:S(2)}, u32[]{:S(2)}) collective-permute-start(bf16[1024,256]{1,0:T(8,128)(2,1)S(1)} %shard_map.92.two), channel_id=1, source_target_pairs={{1,0},{3,2},{4,5},{6,7},{9,8},{11,10},{12,13},{14,15},{17,16},{19,... | collective-permute-start | bytes 1572872 | tf_op jit(solution)/shard_map/ppermute | solution.py:435
  117.2 10.8 %collective-permute-start.28 = (bf16[256,1024]{1,0:T(8,128)(2,1)S(1)}, bf16[256,1024]{1,0:T(8,128)(2,1)S(1)}, u32[]{:S(2)}, u32[]{:S(2)}) collective-permute-start(bf16[256,1024]{1,0:T(8,128)(2,1)S(1)} %get-tuple-element.27.refs_2_), channel_id=1, source_target_pairs={{4,1},{6,3},{9,12},{11,14},{20,17},{22,19},{25,28},{27,30}} | collective-permute-start | bytes 1572872 | tf_op jit(solution)/shard_map/ppermute | solution.py:471
  120.8 34.1 %collective-permute-start.25 = (bf16[1024,768]{1,0:T(8,128)(2,1)S(1)}, bf16[1024,768]{1,0:T(8,128)(2,1)S(1)}, u32[]{:S(2)}, u32[]{:S(2)}) collective-permute-start(bf16[1024,768]{1,0:T(8,128)(2,1)S(1)} %get-tuple-element.34), channel_id=1, source_target_pairs={{3,1},{6,4},{4,6},{11,9},{9,11},{12,14},{19,17},{22,20},{20,22},{2... | collective-permute-start | bytes 4718600 | tf_op jit(solution)/shard_map/ppermute | solution.py:435
  123.2 6.4 %collective-permute-start.27 = (bf16[256,1024]{1,0:T(8,128)(2,1)S(1)}, bf16[256,1024]{1,0:T(8,128)(2,1)S(1)}, u32[]{:S(2)}, u32[]{:S(2)}) collective-permute-start(bf16[256,1024]{1,0:T(8,128)(2,1)S(1)} %get-tuple-element.27.refs_2_), channel_id=1, source_target_pairs={{5,1},{7,3},{8,12},{10,14},{21,17},{23,19},{24,28},{26,30}} | collective-permute-start | bytes 1572872 | tf_op jit(solution)/shard_map/ppermute | solution.py:471
  125.6 13.9 %collective-permute-start.31 = (bf16[256,1024]{1,0:T(8,128)(2,1)S(1)}, bf16[256,1024]{1,0:T(8,128)(2,1)S(1)}, u32[]{:S(2)}, u32[]{:S(2)}) collective-permute-start(bf16[256,1024]{1,0:T(8,128)(2,1)S(1)} %get-tuple-element.28.refs_3_), channel_id=1, source_target_pairs={{4,1},{6,3},{9,12},{11,14},{20,17},{22,19},{25,28},{27,30}} | collective-permute-start | bytes 1572872 | tf_op jit(solution)/shard_map/ppermute | solution.py:471
  127.2 21.5 %collective-permute-start.20 = (bf16[1024,512]{1,0:T(8,128)(2,1)S(1)}, bf16[1024,512]{1,0:T(8,128)(2,1)S(1)}, u32[]{:S(2)}, u32[]{:S(2)}) collective-permute-start(bf16[1024,512]{1,0:T(8,128)(2,1)S(1)} %get-tuple-element.30), channel_id=1, source_target_pairs={{0,2},{2,0},{5,7},{7,5},{10,8},{8,10},{15,13},{13,15},{16,18},{18,... | collective-permute-start | bytes 3145736 | tf_op jit(solution)/shard_map/ppermute | solution.py:435
  128.0 12.2 %collective-permute-start.30 = (bf16[256,1024]{1,0:T(8,128)(2,1)S(1)}, bf16[256,1024]{1,0:T(8,128)(2,1)S(1)}, u32[]{:S(2)}, u32[]{:S(2)}) collective-permute-start(bf16[256,1024]{1,0:T(8,128)(2,1)S(1)} %get-tuple-element.28.refs_3_), channel_id=1, source_target_pairs={{5,1},{7,3},{8,12},{10,14},{21,17},{23,19},{24,28},{26,30}} | collective-permute-start | bytes 1572872 | tf_op jit(solution)/shard_map/ppermute | solution.py:471
  129.6 12.6 %collective-permute-start.22 = (bf16[1024,256]{1,0:T(8,128)(2,1)S(1)}, bf16[1024,256]{1,0:T(8,128)(2,1)S(1)}, u32[]{:S(2)}, u32[]{:S(2)}) collective-permute-start(bf16[1024,256]{1,0:T(8,128)(2,1)S(1)} %get-tuple-element.32), channel_id=1, source_target_pairs={{0,2},{2,0},{5,7},{7,5},{10,8},{8,10},{15,13},{13,15},{16,18},{18,... | collective-permute-start | bytes 1572872 | tf_op jit(solution)/shard_map/ppermute | solution.py:435
  139.5 22.8 %collective-permute-start.29 = (bf16[1024,256]{1,0:T(8,128)(2,1)S(1)}, bf16[1024,256]{1,0:T(8,128)(2,1)S(1)}, u32[]{:S(2)}, u32[]{:S(2)}) collective-permute-start(bf16[1024,256]{1,0:T(8,128)(2,1)S(1)} %shard_map.98.refs_0_.end_a), channel_id=1, source_target_pairs={{1,3},{14,12},{17,19},{30,28}} | collective-permute-start | bytes 1572872 | tf_op jit(solution)/shard_map/ppermute | solution.py:435
  141.5 21.6 %collective-permute-start.32 = (bf16[1024,256]{1,0:T(8,128)(2,1)S(1)}, bf16[1024,256]{1,0:T(8,128)(2,1)S(1)}, u32[]{:S(2)}, u32[]{:S(2)}) collective-permute-start(bf16[1024,256]{1,0:T(8,128)(2,1)S(1)} %shard_map.99.refs_2_.end_b), channel_id=1, source_target_pairs={{1,3},{14,12},{17,19},{30,28}} | collective-permute-start | bytes 1572872 | tf_op jit(solution)/shard_map/ppermute | solution.py:435
  142.2 24.2 %collective-permute-start.12 = (bf16[256,1024]{1,0:T(8,128)(2,1)S(1)}, bf16[256,1024]{1,0:T(8,128)(2,1)S(1)}, u32[]{:S(2)}, u32[]{:S(2)}) collective-permute-start(bf16[256,1024]{1,0:T(8,128)(2,1)S(1)} %shard_map.86.refs_2_), channel_id=1, source_target_pairs={{4,1},{6,3},{9,12},{11,14},{20,17},{22,19},{25,28},{27,30}} | collective-permute-start | bytes 1572872 | tf_op jit(solution)/shard_map/ppermute | solution.py:471
  148.8 18.2 %collective-permute-start.11 = (bf16[256,1024]{1,0:T(8,128)(2,1)S(1)}, bf16[256,1024]{1,0:T(8,128)(2,1)S(1)}, u32[]{:S(2)}, u32[]{:S(2)}) collective-permute-start(bf16[256,1024]{1,0:T(8,128)(2,1)S(1)} %shard_map.86.refs_2_), channel_id=1, source_target_pairs={{5,1},{7,3},{8,12},{10,14},{21,17},{23,19},{24,28},{26,30}} | collective-permute-start | bytes 1572872 | tf_op jit(solution)/shard_map/ppermute | solution.py:471
  154.9 10.7 %collective-permute-start.2 = (f32[8,512]{1,0:T(8,128)S(1)}, f32[8,512]{1,0:T(8,128)S(1)}, u32[]{:S(2)}, u32[]{:S(2)}) collective-permute-start(f32[8,512]{1,0:T(8,128)S(1)} %get-tuple-element.20), channel_id=1, source_target_pairs={{0,1},{1,0},{2,3},{3,2},{4,5},{5,4},{6,7},{7,6},{8,9},{9,8},{10,11... | collective-permute-start | bytes 49160 | tf_op jit(solution)/shard_map/ppermute | solution.py:526
  162.3 9.2 %collective-permute-start.23 = (bf16[512,768]{1,0:T(8,128)(2,1)S(1)}, bf16[512,768]{1,0:T(8,128)(2,1)S(1)}, u32[]{:S(2)}, u32[]{:S(2)}) collective-permute-start(bf16[512,768]{1,0:T(8,128)(2,1)S(1)} %shard_map.94), channel_id=1, source_target_pairs={{2,18},{7,23},{8,24},{13,29},{18,2},{23,7},{24,8},{29,13}} | collective-permute-start | bytes 2359304 | tf_op jit(solution)/shard_map/ppermute | solution.py:605
  163.0 20.6 %collective-permute-start.26 = (bf16[512,768]{1,0:T(8,128)(2,1)S(1)}, bf16[512,768]{1,0:T(8,128)(2,1)S(1)}, u32[]{:S(2)}, u32[]{:S(2)}) collective-permute-start(bf16[512,768]{1,0:T(8,128)(2,1)S(1)} %shard_map.97), channel_id=1, source_target_pairs={{1,17},{4,20},{6,22},{9,25},{11,27},{14,30},{17,1},{20,4},{22,6},{... | collective-permute-start | bytes 2359304 | tf_op jit(solution)/shard_map/ppermute | solution.py:605
  168.3 17.9 %collective-permute-start.13 = (bf16[512,256]{1,0:T(8,128)(2,1)S(1)}, bf16[512,256]{1,0:T(8,128)(2,1)S(1)}, u32[]{:S(2)}, u32[]{:S(2)}) collective-permute-start(bf16[512,256]{1,0:T(8,128)(2,1)S(1)} %get-tuple-element.24.kept), channel_id=1, source_target_pairs={{1,3},{14,12},{17,19},{30,28}} | collective-permute-start | bytes 786440 | tf_op jit(solution)/shard_map/ppermute | solution.py:435
  170.2 16.0 %collective-permute-start.15 = (bf16[512,256]{1,0:T(8,128)(2,1)S(1)}, bf16[512,256]{1,0:T(8,128)(2,1)S(1)}, u32[]{:S(2)}, u32[]{:S(2)}) collective-permute-start(bf16[512,256]{1,0:T(8,128)(2,1)S(1)} %get-tuple-element.25), channel_id=1, source_target_pairs={{3,19},{12,28},{19,3},{28,12}} | collective-permute-start | bytes 786440 | tf_op jit(solution)/shard_map/ppermute | solution.py:605
  170.9 15.3 %collective-permute-start.14 = (bf16[512,256]{1,0:T(8,128)(2,1)S(1)}, bf16[512,256]{1,0:T(8,128)(2,1)S(1)}, u32[]{:S(2)}, u32[]{:S(2)}) collective-permute-start(bf16[512,256]{1,0:T(8,128)(2,1)S(1)} %get-tuple-element.25), channel_id=1, source_target_pairs={{1,19},{14,28},{17,3},{30,12}} | collective-permute-start | bytes 786440 | tf_op jit(solution)/shard_map/ppermute | solution.py:605
  (11 other events, 107.0 us)
where the time goes:
time: 188 us; the launch traced here: 187 us
  waiting for transfers between devices  83.8 us (45%)
  starting transfers between devices  62.2 us (33%)
  Pallas kernels  38.1 us (20%)
  local copies, waits for them, and re-layouts  1.93 us (1%)
    ppermute x2, waiting for transfers between devices, shards_grid(): low = [lax.ppermute(low_a, 'seq', up), lax.ppermute(low_b, 'seq', up)]  24.8 us
    ppermute x2, waiting for transfers between devices, shards_grid(): low2 = [lax.ppermute(low[n], 'seq', up[1:]) for n in range(2)]  15.4 us
    ppermute x12, starting transfers between devices, across(): lax.ppermute(value, ('seq', 'head'), [(b * count + h, b * count + k) for...  13.7 us
    pallas_call x4, Pallas kernels, product(): pl.pallas_call(functools.partial(product_kernel, lefts=len(lefts), weight...  12.8 us
    ppermute x5, waiting for transfers between devices, anywhere(): return lax.ppermute(value, ('groups', 'seq', 'head'), flat)  12.2 us
    ppermute x6, starting transfers between devices, shards_grid(): lax.ppermute(part, ('seq', 'head'), [(b * count + (h ^ turn), end * count...  11.6 us
    ppermute x1, waiting for transfers between devices, shards_grid(): high2 = lax.ppermute(high, 'seq', down[:-1])  9.36 us
    ppermute x6, waiting for transfers between devices, shards_grid(): lax.ppermute(part, ('seq', 'head'), [(b * count + (h ^ turn), end * count...  7.9 us
  transfers between devices with their start and end apart: 34, of which 9 were waited for; matrix products, arithmetic and copies ran while one was open for 0% of the time, Pallas kernels for 17%

commit v1 on v0

--- a/solution.py
+++ b/solution.py
@@ -312,8 +312,9 @@
 
 
 def most_kernel(
-    where, squares, squares_more, kept_a, more_a, kept_b, more_b, back, near, near_more, near_back,
-    end_a, end_a_more, end_b, end_b_more, end_back, out, one, two, sems, *, width, count
+    where, squares, squares_more, kept_a, more_a, back_a, kept_b, more_b, back_b, near, near_more, near_back,
+    end_a, end_a_more, end_a_back, end_b, end_b_more, end_b_across, end_b_back, out, one, two, sems,
+    *, width, count
 ):
     rows, full = out.shape
     half = full // 2
@@ -351,7 +352,8 @@
             (more_a.at[low], two.at[low, most]),
             (kept_b.at[low], one.at[low, others]),
             (more_b.at[low], two.at[low, others]),
-            (back, one.at[high]),
+            (back_a, one.at[high, most]),
+            (back_b, one.at[high, others]),
         )
 
     @pl.when(beside)
@@ -371,7 +373,9 @@
             (end_b.at[low], one.at[low, second]),
             (end_a_more.at[low], two.at[low, first]),
             (end_b_more.at[low], two.at[low, second]),
-            (end_back, one.at[high, most]),
+            (end_a_back, one.at[high, first]),
+            (end_b_across, one.at[high, second]),
+            (end_b_back, two.at[high, second]),
         )
 
     for group in range(2):
@@ -385,7 +389,8 @@
         @pl.when(end & (where[1] == group))
         def _(this=this):
             put(this, one[low, : 2 * cut], two[low, : 2 * cut])
-            put(half - this, one[high, : 2 * cut])
+            put(half - this, one[high, :cut])
+            put(half - this + cut, one[high, cut : 2 * cut], two[high, cut : 2 * cut])
 
 
 def last_kernel(
@@ -624,37 +629,41 @@
         two = (made, from_core(made, {b: b ^ 2 for b in index}))
         kept, sent = pair(own, two, 2 * n * cut)
         more = across(sent, [(b, h, h ^ 2) for b in index for h in (b, b ^ 2)])
-        pieces.append((kept, more))
-    back = give_back(add(*pieces, part=1, parts=2), [(b, b ^ 2) for b in index])
+        total = add((kept, more), part=1, parts=2)
+        back = give_back(total, [(b, b ^ 2) for b in index])
+        pieces += [kept, more, back]
 
     last = []
     for n, part in enumerate(far3):
-        parts = 1 if n < 2 else 2
+        parts = 1 if n == 0 else 2
         made = pl.pallas_call(
             end_kernel,
             out_shape=[pltpu.VMEM((2 * tok_rows // parts, cut), jnp.bfloat16)] * parts,
             compiler_params=limit(12),
             cost_estimate=cost(8 * tok_rows * cut * wide, 8),
         )(gated, other, *turned, *part)
-        last.append((made[0], across(made[0], [(b, f ^ 2, f) for b, f in ends.items()])))
-    first_back = give_back(add(*last[:2], part=1, parts=2), ends.items())
-    pairs = [((g, b, f ^ 2), (1 - g, b, f)) for g in range(2) for b, f in ends.items()]
-    last_back = anywhere(made[1], pairs), give_back(made[1], ends.items())
+        last += [made[0], across(made[0], [(b, f ^ 2, f) for b, f in ends.items()])]
+        if parts == 1:
+            total = add(tuple(last), part=1, parts=2)
+            last.append(give_back(total, ends.items()))
+        else:
+            pairs = [((g, b, f ^ 2), (1 - g, b, f)) for g in range(2) for b, f in ends.items()]
+            last += [anywhere(made[1], pairs), give_back(made[1], ends.items())]
 
     sizes = {"width": wide * count, "count": count}
     most = pl.pallas_call(
         functools.partial(most_kernel, **sizes),
-        in_specs=[SMEM, pl.BlockSpec(), pl.BlockSpec()] + [ANY] * 13,
+        in_specs=[SMEM, pl.BlockSpec(), pl.BlockSpec()] + [ANY] * 16,
         out_shape=table((tok_rows, 2 * half), jnp.bfloat16),
         scratch_shapes=[
             pltpu.VMEM((2 * tok_rows, half), jnp.bfloat16),
             pltpu.VMEM((2 * tok_rows, half), jnp.bfloat16),
-            pltpu.SemaphoreType.DMA((6,)),
+            pltpu.SemaphoreType.DMA((7,)),
         ],
         compiler_params=limit(8),
     )(
-        where, squares, squares_more, *pieces[0], *pieces[1], back,
-        near_kept, near_more, near_back, *last[0], *last[1], first_back,
+        where, squares, squares_more, *pieces,
+        near_kept, near_more, near_back, *last[:7],
     )
     return pl.pallas_call(
         functools.partial(last_kernel, **sizes),
@@ -668,7 +677,7 @@
         ],
         input_output_aliases={7: 0},
         compiler_params=limit(4),
-    )(where, squares, squares_more, *last[2], *last_back, most)
+    )(where, squares, squares_more, *last[7:], most)
 
 
 def shards_general(

time: 188 us -> 193 us (1.027)
  the two profiles are of different devices: /device:TPU:14 before, /device:TPU:28 now
where the time goes in v1:
time: 193 us; the launch traced here: 192 us
  waiting for transfers between devices  98.2 us (51%)
  starting transfers between devices  51.7 us (27%)
  Pallas kernels  39.3 us (20%)
  local copies, waits for them, and re-layouts  1.93 us (1%)
    ppermute x2, waiting for transfers between devices, shards_grid(): low = [lax.ppermute(low_a, 'seq', up), lax.ppermute(low_b, 'seq', up)]  26.7 us
    ppermute x2, waiting for transfers between devices, shards_grid(): low2 = [lax.ppermute(low[n], 'seq', up[1:]) for n in range(2)]  25.5 us
    ppermute x6, waiting for transfers between devices, shards_grid(): lax.ppermute(part, ('seq', 'head'), [(b * count + (h ^ turn), end * count...  21.3 us
    ppermute x12, starting transfers between devices, across(): lax.ppermute(value, ('seq', 'head'), [(b * count + h, b * count + k) for...  17.6 us
    ppermute x8, starting transfers between devices, anywhere(): return lax.ppermute(value, ('groups', 'seq', 'head'), flat)  12.9 us
    pallas_call x4, Pallas kernels, product(): pl.pallas_call(functools.partial(product_kernel, lefts=len(lefts), weight...  12.8 us
    ppermute x8, waiting for transfers between devices, anywhere(): return lax.ppermute(value, ('groups', 'seq', 'head'), flat)  8.85 us
    ppermute x6, starting transfers between devices, shards_grid(): lax.ppermute(part, ('seq', 'head'), [(b * count + (h ^ turn), end * count...  7.72 us
  transfers between devices with their start and end apart: 37, of which 15 were waited for; matrix products, arithmetic and copies ran while one was open for 0% of the time, Pallas kernels for 16%

profile of v1, /device:TPU:28, one launch (start us, length us, event | category | flops | bytes accessed | tf_op | source)
XLA Modules:
  0.0 192.1 jit_solution(13242276659140737602)
XLA Ops:
  0.1 1.9 copy-done.3
  2.8 2.6 %collective-permute-start.9 = (bf16[768,1024]{1,0:T(8,128)(2,1)S(1)}, bf16[768,1024]{1,0:T(8,128)(2,1)S(1)}, u32[]{:S(2)}, u32[]{:S(2)}) collective-permute-start(bf16[768,1024]{1,0:T(8,128)(2,1)S(1)} %get-tuple-element.25), channel_id=1, source_target_pairs={{4,0},{8,4},{12,8},{5,1},{9,5},{13,9},{6,2},{10,6},{14,10},{7,3},{... | collective-permute-start | bytes 4718600 | tf_op jit(solution)/shard_map/ppermute | solution.py:458
  5.4 2.4 %shard_map.83 = bf16[8,128,128]{2,1,0:T(8,128)(2,1)S(1)} custom-call(s32[3]{0:T(128)S(1)} %pad_add_fusion.where, s32[4]{0:T(128)S(1)} %copy-done.6, s32[8]{0:T(128)S(1)} %copy-done.7, bf16[512,1024]{1,0:T(8,128)(2,1)S(1)} %copy-done, bf16[512,1024]{1,0:T(8,128)(2,1)S(1)} %copy-done.1), custom_call_target="tpu_custom_call" | custom-call | tf_op jit(solution)/shard_map/pallas_call | solution.py:493
  11.8 5.1 %shard_map.82.intra = f32[512,1024]{1,0:T(8,128)S(1)} custom-call(s32[3]{0:T(128)S(1)} %pad_add_fusion.where, s32[4]{0:T(128)S(1)} %copy-done.6, s32[8]{0:T(128)S(1)} %copy-done.7, bf16[512,1024]{1,0:T(8,128)(2,1)S(1)} %copy-done.2, bf16[512,1024]{1,0:T(8,128)(2,1)S(1)} %copy-done, bf16[512,1024]{1,0:T(8,128)(2,1)S(1)} %copy-done.1), custom_call_target="tpu_custom_call" | custom-call | tf_op jit(solution)/shard_map/pallas_call | solution.py:503
  16.9 7.1 %collective-permute-done.1.far = bf16[8,128,128]{2,1,0:T(8,128)(2,1)S(1)} collective-permute-done((bf16[8,128,128]{2,1,0:T(8,128)(2,1)S(1)}, bf16[8,128,128]{2,1,0:T(8,128)(2,1)S(1)}, u32[]{:S(2)}, u32[]{:S(2)}) %collective-permute-start.1) | collective-permute-done | bytes 262176 | tf_op jit(solution)/shard_map/ppermute | solution.py:502
  24.0 1.8 collective-permute-done.near
  25.8 3.6 %shard_map.84 = (bf16[512,1024]{1,0:T(8,128)(2,1)S(1)}, f32[8,512]{1,0:T(8,128)S(1)}) custom-call(s32[3]{0:T(128)S(1)} %pad_add_fusion.where, s32[4]{0:T(128)S(1)} %copy-done.6, s32[8]{0:T(128)S(1)} %copy-done.7, bf16[512,1024]{1,0:T(8,128)(2,1)S(1)} %copy-done.2, f32[512,1024]{1,0:T(8,128)S(1)} %shard_map.82.intra, ...), custom_call_target="tpu_custom_call" | custom-call | tf_op jit(solution)/shard_map/pallas_call | solution.py:511
  31.5 26.7 %collective-permute-done.7.refs_3_ = bf16[256,1024]{1,0:T(8,128)(2,1)S(1)} collective-permute-done((bf16[256,1024]{1,0:T(8,128)(2,1)S(1)}, bf16[256,1024]{1,0:T(8,128)(2,1)S(1)}, u32[]{:S(2)}, u32[]{:S(2)}) %collective-permute-start.7) | collective-permute-done | bytes 524320 | tf_op jit(solution)/shard_map/ppermute | solution.py:457
  58.1 5.8 %shard_map.96.made = bf16[1024,1536]{1,0:T(8,128)(2,1)S(1)} custom-call(bf16[512,1024]{1,0:T(8,128)(2,1)S(1)} %get-tuple-element.23.own.refs_0_, bf16[512,1024]{1,0:T(8,128)(2,1)S(1)} %collective-permute-done.4.other.refs_1_, bf16[512,1024]{1,0:T(8,128)(2,1)S(1)} %collective-permute-done.17.refs_2_, bf16[256,1024]{1,0:T(8,128)(2,1)S(1)} %collective-permute-done.7.refs_3_, ...), custom_call_target="tpu_custom_call" | custom-call | flops 3221225472 | bytes 8388608 | tf_op jit(solution)/shard_map/pallas_call | solution.py:537
  67.3 4.6 %shard_map.88.own = bf16[1024,768]{1,0:T(8,128)(2,1)S(1)} custom-call(bf16[512,1024]{1,0:T(8,128)(2,1)S(1)} %get-tuple-element.23.own.refs_0_, bf16[1536,1024]{1,0:T(8,128)(2,1)S(1)} %copy-done.4), custom_call_target="tpu_custom_call" | custom-call | flops 1610612736 | bytes 8388608 | tf_op jit(solution)/shard_map/pallas_call | solution.py:537
  71.9 3.3 %collective-permute-start.16 = (bf16[1024,768]{1,0:T(8,128)(2,1)S(1)}, bf16[1024,768]{1,0:T(8,128)(2,1)S(1)}, u32[]{:S(2)}, u32[]{:S(2)}) collective-permute-start(bf16[1024,768]{1,0:T(8,128)(2,1)S(1)} %shard_map.88.own), channel_id=1, source_target_pairs={{1,0},{3,2},{4,5},{6,7},{9,8},{11,10},{12,13},{14,15},{17,16},{19,... | collective-permute-start | bytes 4718600 | tf_op jit(solution)/shard_map/ppermute | solution.py:440
  75.3 2.9 %collective-permute-done.2 = f32[8,512]{1,0:T(8,128)S(1)} collective-permute-done((f32[8,512]{1,0:T(8,128)S(1)}, f32[8,512]{1,0:T(8,128)S(1)}, u32[]{:S(2)}, u32[]{:S(2)}) %collective-permute-start.2) | collective-permute-done | bytes 16416 | tf_op jit(solution)/shard_map/ppermute | solution.py:531
  78.6 20.1 %collective-permute-done.18.low = bf16[512,1024]{1,0:T(8,128)(2,1)S(1)} collective-permute-done((bf16[512,1024]{1,0:T(8,128)(2,1)S(1)}, bf16[512,1024]{1,0:T(8,128)(2,1)S(1)}, u32[]{:S(2)}, u32[]{:S(2)}) %collective-permute-start.18) | collective-permute-done | bytes 1048608 | tf_op jit(solution)/shard_map/ppermute | solution.py:459
  100.0 1.6 collective-permute-start.3
  102.4 1.6 shard_map.90.two
  104.1 2.4 %collective-permute-start.19 = (bf16[1024,512]{1,0:T(8,128)(2,1)S(1)}, bf16[1024,512]{1,0:T(8,128)(2,1)S(1)}, u32[]{:S(2)}, u32[]{:S(2)}) collective-permute-start(bf16[1024,512]{1,0:T(8,128)(2,1)S(1)} %shard_map.90.two), channel_id=1, source_target_pairs={{1,0},{3,2},{4,5},{6,7},{9,8},{11,10},{12,13},{14,15},{17,16},{19,... | collective-permute-start | bytes 3145736 | tf_op jit(solution)/shard_map/ppermute | solution.py:440
  106.5 2.2 %shard_map.97 = (bf16[1024,768]{1,0:T(8,128)(2,1)S(1)}, bf16[1024,768]{1,0:T(8,128)(2,1)S(1)}) custom-call(s32[3]{0:T(128)S(1)} %pad_add_fusion.where, bf16[1024,1536]{1,0:T(8,128)(2,1)S(1)} %shard_map.96.made, bf16[1024,1536]{1,0:T(8,128)(2,1)S(1)} %collective-permute-done.25.come), custom_call_target="tpu_custom_call" | custom-call | flops 1572864 | bytes 9437184 | tf_op jit(solution)/shard_map/pallas_call | solution.py:561
  108.8 5.4 %collective-permute-done.8.low = bf16[256,1024]{1,0:T(8,128)(2,1)S(1)} collective-permute-done((bf16[256,1024]{1,0:T(8,128)(2,1)S(1)}, bf16[256,1024]{1,0:T(8,128)(2,1)S(1)}, u32[]{:S(2)}, u32[]{:S(2)}) %collective-permute-start.8) | collective-permute-done | bytes 524320 | tf_op jit(solution)/shard_map/ppermute | solution.py:459
  114.2 3.5 %collective-permute-start.26 = (bf16[1024,768]{1,0:T(8,128)(2,1)S(1)}, bf16[1024,768]{1,0:T(8,128)(2,1)S(1)}, u32[]{:S(2)}, u32[]{:S(2)}) collective-permute-start(bf16[1024,768]{1,0:T(8,128)(2,1)S(1)} %get-tuple-element.36), channel_id=1, source_target_pairs={{3,1},{6,4},{4,6},{11,9},{9,11},{12,14},{19,17},{22,20},{20,22},{2... | collective-permute-start | bytes 4718600 | tf_op jit(solution)/shard_map/ppermute | solution.py:440
  124.4 1.6 shard_map.91
  126.7 8.0 %collective-permute-done.29.weight_turned = bf16[256,1024]{1,0:T(8,128)(2,1)S(1)} collective-permute-done((bf16[256,1024]{1,0:T(8,128)(2,1)S(1)}, bf16[256,1024]{1,0:T(8,128)(2,1)S(1)}, u32[]{:S(2)}, u32[]{:S(2)}) %collective-permute-start.29) | collective-permute-done | bytes 524320 | tf_op jit(solution)/shard_map/ppermute | solution.py:476
  136.9 1.5 collective-permute-done.28.weight
  139.7 4.5 %collective-permute-done.33.weight_turned = bf16[256,1024]{1,0:T(8,128)(2,1)S(1)} collective-permute-done((bf16[256,1024]{1,0:T(8,128)(2,1)S(1)}, bf16[256,1024]{1,0:T(8,128)(2,1)S(1)}, u32[]{:S(2)}, u32[]{:S(2)}) %collective-permute-start.33) | collective-permute-done | bytes 524320 | tf_op jit(solution)/shard_map/ppermute | solution.py:476
  144.9 6.4 %collective-permute-done.32.weight = bf16[256,1024]{1,0:T(8,128)(2,1)S(1)} collective-permute-done((bf16[256,1024]{1,0:T(8,128)(2,1)S(1)}, bf16[256,1024]{1,0:T(8,128)(2,1)S(1)}, u32[]{:S(2)}, u32[]{:S(2)}) %collective-permute-start.32) | collective-permute-done | bytes 524320 | tf_op jit(solution)/shard_map/ppermute | solution.py:476
  158.8 2.4 %collective-permute-start.36 = (bf16[512,256]{1,0:T(8,128)(2,1)S(1)}, bf16[512,256]{1,0:T(8,128)(2,1)S(1)}, u32[]{:S(2)}, u32[]{:S(2)}) collective-permute-start(bf16[512,256]{1,0:T(8,128)(2,1)S(1)} %get-tuple-element.38), channel_id=1, source_target_pairs={{3,19},{12,28},{19,3},{28,12}} | collective-permute-start | bytes 786440 | tf_op jit(solution)/shard_map/ppermute | solution.py:610
  163.7 4.1 %collective-permute-done.34.end_b_more = bf16[512,256]{1,0:T(8,128)(2,1)S(1)} collective-permute-done((bf16[512,256]{1,0:T(8,128)(2,1)S(1)}, bf16[512,256]{1,0:T(8,128)(2,1)S(1)}, u32[]{:S(2)}, u32[]{:S(2)}) %collective-permute-start.34) | collective-permute-done | bytes 262176 | tf_op jit(solution)/shard_map/ppermute | solution.py:440
  169.3 3.4 %collective-permute-done.36.end_b_back = bf16[512,256]{1,0:T(8,128)(2,1)S(1)} collective-permute-done((bf16[512,256]{1,0:T(8,128)(2,1)S(1)}, bf16[512,256]{1,0:T(8,128)(2,1)S(1)}, u32[]{:S(2)}, u32[]{:S(2)}) %collective-permute-start.36) | collective-permute-done | bytes 262176 | tf_op jit(solution)/shard_map/ppermute | solution.py:610
  172.7 2.4 %collective-permute-start.31 = (bf16[512,256]{1,0:T(8,128)(2,1)S(1)}, bf16[512,256]{1,0:T(8,128)(2,1)S(1)}, u32[]{:S(2)}, u32[]{:S(2)}) collective-permute-start(bf16[512,256]{1,0:T(8,128)(2,1)S(1)} %shard_map.100), channel_id=1, source_target_pairs={{3,19},{12,28},{19,3},{28,12}} | collective-permute-start | bytes 786440 | tf_op jit(solution)/shard_map/ppermute | solution.py:610
  177.7 3.4 %collective-permute-start.15 = (bf16[512,256]{1,0:T(8,128)(2,1)S(1)}, bf16[512,256]{1,0:T(8,128)(2,1)S(1)}, u32[]{:S(2)}, u32[]{:S(2)}) collective-permute-start(bf16[512,256]{1,0:T(8,128)(2,1)S(1)} %get-tuple-element.27), channel_id=1, source_target_pairs={{3,19},{12,28},{19,3},{28,12}} | collective-permute-start | bytes 786440 | tf_op jit(solution)/shard_map/ppermute | solution.py:610
  182.5 2.4 %shard_map.102.most = bf16[512,1536]{1,0:T(8,128)(2,1)} custom-call(s32[3]{0:T(128)S(1)} %pad_add_fusion.where, f32[8,512]{1,0:T(8,128)S(1)} %add.3.squares, f32[8,512]{1,0:T(8,128)S(1)} %collective-permute-done.3.squares_more, bf16[1024,512]{1,0:T(8,128)(2,1)S(1)} %get-tuple-element.31.refs_0_.kept_a, ...), custom_call_target="tpu_custom_call" | custom-call | tf_op jit(solution)/shard_map/pallas_call | solution.py:654
  186.0 4.4 %collective-permute-done.14.across = bf16[512,256]{1,0:T(8,128)(2,1)S(1)} collective-permute-done((bf16[512,256]{1,0:T(8,128)(2,1)S(1)}, bf16[512,256]{1,0:T(8,128)(2,1)S(1)}, u32[]{:S(2)}, u32[]{:S(2)}) %collective-permute-start.14) | collective-permute-done | bytes 262176 | tf_op jit(solution)/shard_map/ppermute | solution.py:610
  190.3 1.7 shard_map.103
  (85 shorter events, 40.7 us)
Async XLA Ops:
  2.8 55.3 %collective-permute-start.9 = (bf16[768,1024]{1,0:T(8,128)(2,1)S(1)}, bf16[768,1024]{1,0:T(8,128)(2,1)S(1)}, u32[]{:S(2)}, u32[]{:S(2)}) collective-permute-start(bf16[768,1024]{1,0:T(8,128)(2,1)S(1)} %get-tuple-element.25), channel_id=1, source_target_pairs={{4,0},{8,4},{12,8},{5,1},{9,5},{13,9},{6,2},{10,6},{14,10},{7,3},{... | collective-permute-start | bytes 4718600 | tf_op jit(solution)/shard_map/ppermute | solution.py:458
  7.9 16.1 %collective-permute-start.1 = (bf16[8,128,128]{2,1,0:T(8,128)(2,1)S(1)}, bf16[8,128,128]{2,1,0:T(8,128)(2,1)S(1)}, u32[]{:S(2)}, u32[]{:S(2)}) collective-permute-start(bf16[8,128,128]{2,1,0:T(8,128)(2,1)S(1)} %shard_map.83), channel_id=1, source_target_pairs={{0,8},{4,12},{1,9},{5,13},{2,10},{6,14},{3,11},{7,15},{16,24},{20,... | collective-permute-start | bytes 786440 | tf_op jit(solution)/shard_map/ppermute | solution.py:502
  9.2 16.6 %collective-permute-start = (bf16[8,128,128]{2,1,0:T(8,128)(2,1)S(1)}, bf16[8,128,128]{2,1,0:T(8,128)(2,1)S(1)}, u32[]{:S(2)}, u32[]{:S(2)}) collective-permute-start(bf16[8,128,128]{2,1,0:T(8,128)(2,1)S(1)} %shard_map.83), channel_id=1, source_target_pairs={{0,4},{4,8},{8,12},{1,5},{5,9},{9,13},{2,6},{6,10},{10,14},{3,7},{... | collective-permute-start | bytes 786440 | tf_op jit(solution)/shard_map/ppermute | solution.py:501
  10.5 47.6 %collective-permute-start.17 = (bf16[512,1024]{1,0:T(8,128)(2,1)S(1)}, bf16[512,1024]{1,0:T(8,128)(2,1)S(1)}, u32[]{:S(2)}, u32[]{:S(2)}) collective-permute-start(bf16[512,1024]{1,0:T(8,128)(2,1)S(1)} %get-tuple-element.28), channel_id=1, source_target_pairs={{0,4},{4,8},{8,12},{1,5},{5,9},{9,13},{2,6},{6,10},{10,14},{3,7},{... | collective-permute-start | bytes 3145736 | tf_op jit(solution)/shard_map/ppermute | solution.py:457
  29.4 28.8 %collective-permute-start.4 = (bf16[512,1024]{1,0:T(8,128)(2,1)S(1)}, bf16[512,1024]{1,0:T(8,128)(2,1)S(1)}, u32[]{:S(2)}, u32[]{:S(2)}) collective-permute-start(bf16[512,1024]{1,0:T(8,128)(2,1)S(1)} %get-tuple-element.23.own.refs_0_), channel_id=1, source_target_pairs={{0,16},{16,0},{1,17},{17,1},{2,18},{18,2},{3,19},{19,3},{4,20},{20... | collective-permute-start | bytes 3145736 | tf_op jit(solution)/shard_map/ppermute | solution.py:526
  29.9 28.2 %collective-permute-start.7 = (bf16[256,1024]{1,0:T(8,128)(2,1)S(1)}, bf16[256,1024]{1,0:T(8,128)(2,1)S(1)}, u32[]{:S(2)}, u32[]{:S(2)}) collective-permute-start(bf16[256,1024]{1,0:T(8,128)(2,1)S(1)} %get-tuple-element.24), channel_id=1, source_target_pairs={{0,4},{4,8},{8,12},{1,5},{5,9},{9,13},{2,6},{6,10},{10,14},{3,7},{... | collective-permute-start | bytes 1572872 | tf_op jit(solution)/shard_map/ppermute | solution.py:457
  63.9 40.2 %collective-permute-start.25 = (bf16[1024,1536]{1,0:T(8,128)(2,1)S(1)}, bf16[1024,1536]{1,0:T(8,128)(2,1)S(1)}, u32[]{:S(2)}, u32[]{:S(2)}) collective-permute-start(bf16[1024,1536]{1,0:T(8,128)(2,1)S(1)} %shard_map.96.made), channel_id=1, source_target_pairs={{0,1},{2,3},{5,4},{7,6},{8,9},{10,11},{13,12},{15,14},{16,17},{18,... | collective-permute-start | bytes 9437192 | tf_op jit(solution)/shard_map/ppermute | solution.py:440
  65.2 34.8 %collective-permute-start.10 = (bf16[768,1024]{1,0:T(8,128)(2,1)S(1)}, bf16[768,1024]{1,0:T(8,128)(2,1)S(1)}, u32[]{:S(2)}, u32[]{:S(2)}) collective-permute-start(bf16[768,1024]{1,0:T(8,128)(2,1)S(1)} %collective-permute-done.9.refs_4_), channel_id=1, source_target_pairs={{4,0},{8,4},{5,1},{9,5},{6,2},{10,6},{7,3},{11,7},{20,16},{24,20},... | collective-permute-start | bytes 4718600 | tf_op jit(solution)/shard_map/ppermute | solution.py:460
  66.0 32.7 %collective-permute-start.18 = (bf16[512,1024]{1,0:T(8,128)(2,1)S(1)}, bf16[512,1024]{1,0:T(8,128)(2,1)S(1)}, u32[]{:S(2)}, u32[]{:S(2)}) collective-permute-start(bf16[512,1024]{1,0:T(8,128)(2,1)S(1)} %collective-permute-done.17.refs_2_), channel_id=1, source_target_pairs={{4,8},{8,12},{5,9},{9,13},{6,10},{10,14},{7,11},{11,15},{20,24},{2... | collective-permute-start | bytes 3145736 | tf_op jit(solution)/shard_map/ppermute | solution.py:459
  71.9 48.5 %collective-permute-start.16 = (bf16[1024,768]{1,0:T(8,128)(2,1)S(1)}, bf16[1024,768]{1,0:T(8,128)(2,1)S(1)}, u32[]{:S(2)}, u32[]{:S(2)}) collective-permute-start(bf16[1024,768]{1,0:T(8,128)(2,1)S(1)} %shard_map.88.own), channel_id=1, source_target_pairs={{1,0},{3,2},{4,5},{6,7},{9,8},{11,10},{12,13},{14,15},{17,16},{19,... | collective-permute-start | bytes 4718600 | tf_op jit(solution)/shard_map/ppermute | solution.py:440
  78.2 40.9 %collective-permute-start.5 = (bf16[512,1024]{1,0:T(8,128)(2,1)S(1)}, bf16[512,1024]{1,0:T(8,128)(2,1)S(1)}, u32[]{:S(2)}, u32[]{:S(2)}) collective-permute-start(bf16[512,1024]{1,0:T(8,128)(2,1)S(1)} %get-tuple-element.23.own.refs_0_), channel_id=1, source_target_pairs={{0,1},{1,0},{2,3},{3,2},{4,5},{5,4},{6,7},{7,6},{8,9},{9,8},{10,11... | collective-permute-start | bytes 3145736 | tf_op jit(solution)/shard_map/ppermute | solution.py:440
  98.7 15.5 %collective-permute-start.8 = (bf16[256,1024]{1,0:T(8,128)(2,1)S(1)}, bf16[256,1024]{1,0:T(8,128)(2,1)S(1)}, u32[]{:S(2)}, u32[]{:S(2)}) collective-permute-start(bf16[256,1024]{1,0:T(8,128)(2,1)S(1)} %collective-permute-done.7.refs_3_), channel_id=1, source_target_pairs={{4,8},{8,12},{5,9},{9,13},{6,10},{10,14},{7,11},{11,15},{20,24},{2... | collective-permute-start | bytes 1572872 | tf_op jit(solution)/shard_map/ppermute | solution.py:459
  104.0 17.8 %collective-permute-start.6 = (bf16[512,1024]{1,0:T(8,128)(2,1)S(1)}, bf16[512,1024]{1,0:T(8,128)(2,1)S(1)}, u32[]{:S(2)}, u32[]{:S(2)}) collective-permute-start(bf16[512,1024]{1,0:T(8,128)(2,1)S(1)} %collective-permute-done.4.other.refs_1_), channel_id=1, source_target_pairs={{0,1},{1,0},{2,3},{3,2},{4,5},{5,4},{6,7},{7,6},{8,9},{9,8},{10,11... | collective-permute-start | bytes 3145736 | tf_op jit(solution)/shard_map/ppermute | solution.py:440
  104.1 19.0 %collective-permute-start.19 = (bf16[1024,512]{1,0:T(8,128)(2,1)S(1)}, bf16[1024,512]{1,0:T(8,128)(2,1)S(1)}, u32[]{:S(2)}, u32[]{:S(2)}) collective-permute-start(bf16[1024,512]{1,0:T(8,128)(2,1)S(1)} %shard_map.90.two), channel_id=1, source_target_pairs={{1,0},{3,2},{4,5},{6,7},{9,8},{11,10},{12,13},{14,15},{17,16},{19,... | collective-permute-start | bytes 3145736 | tf_op jit(solution)/shard_map/ppermute | solution.py:440
  114.2 39.7 %collective-permute-start.26 = (bf16[1024,768]{1,0:T(8,128)(2,1)S(1)}, bf16[1024,768]{1,0:T(8,128)(2,1)S(1)}, u32[]{:S(2)}, u32[]{:S(2)}) collective-permute-start(bf16[1024,768]{1,0:T(8,128)(2,1)S(1)} %get-tuple-element.36), channel_id=1, source_target_pairs={{3,1},{6,4},{4,6},{11,9},{9,11},{12,14},{19,17},{22,20},{20,22},{2... | collective-permute-start | bytes 4718600 | tf_op jit(solution)/shard_map/ppermute | solution.py:440
  120.4 14.2 %collective-permute-start.29 = (bf16[256,1024]{1,0:T(8,128)(2,1)S(1)}, bf16[256,1024]{1,0:T(8,128)(2,1)S(1)}, u32[]{:S(2)}, u32[]{:S(2)}) collective-permute-start(bf16[256,1024]{1,0:T(8,128)(2,1)S(1)} %get-tuple-element.29.refs_2_), channel_id=1, source_target_pairs={{4,1},{6,3},{9,12},{11,14},{20,17},{22,19},{25,28},{27,30}} | collective-permute-start | bytes 1572872 | tf_op jit(solution)/shard_map/ppermute | solution.py:476
  121.7 16.7 %collective-permute-start.28 = (bf16[256,1024]{1,0:T(8,128)(2,1)S(1)}, bf16[256,1024]{1,0:T(8,128)(2,1)S(1)}, u32[]{:S(2)}, u32[]{:S(2)}) collective-permute-start(bf16[256,1024]{1,0:T(8,128)(2,1)S(1)} %get-tuple-element.29.refs_2_), channel_id=1, source_target_pairs={{5,1},{7,3},{8,12},{10,14},{21,17},{23,19},{24,28},{26,30}} | collective-permute-start | bytes 1572872 | tf_op jit(solution)/shard_map/ppermute | solution.py:476
  123.1 21.2 %collective-permute-start.33 = (bf16[256,1024]{1,0:T(8,128)(2,1)S(1)}, bf16[256,1024]{1,0:T(8,128)(2,1)S(1)}, u32[]{:S(2)}, u32[]{:S(2)}) collective-permute-start(bf16[256,1024]{1,0:T(8,128)(2,1)S(1)} %get-tuple-element.30.refs_3_), channel_id=1, source_target_pairs={{4,1},{6,3},{9,12},{11,14},{20,17},{22,19},{25,28},{27,30}} | collective-permute-start | bytes 1572872 | tf_op jit(solution)/shard_map/ppermute | solution.py:476
  126.0 32.8 %collective-permute-start.20 = (bf16[1024,512]{1,0:T(8,128)(2,1)S(1)}, bf16[1024,512]{1,0:T(8,128)(2,1)S(1)}, u32[]{:S(2)}, u32[]{:S(2)}) collective-permute-start(bf16[1024,512]{1,0:T(8,128)(2,1)S(1)} %get-tuple-element.32), channel_id=1, source_target_pairs={{0,2},{2,0},{5,7},{7,5},{10,8},{8,10},{15,13},{13,15},{16,18},{18,... | collective-permute-start | bytes 3145736 | tf_op jit(solution)/shard_map/ppermute | solution.py:440
  134.7 16.7 %collective-permute-start.32 = (bf16[256,1024]{1,0:T(8,128)(2,1)S(1)}, bf16[256,1024]{1,0:T(8,128)(2,1)S(1)}, u32[]{:S(2)}, u32[]{:S(2)}) collective-permute-start(bf16[256,1024]{1,0:T(8,128)(2,1)S(1)} %get-tuple-element.30.refs_3_), channel_id=1, source_target_pairs={{5,1},{7,3},{8,12},{10,14},{21,17},{23,19},{24,28},{26,30}} | collective-permute-start | bytes 1572872 | tf_op jit(solution)/shard_map/ppermute | solution.py:476
  138.4 18.3 %collective-permute-start.12 = (bf16[256,1024]{1,0:T(8,128)(2,1)S(1)}, bf16[256,1024]{1,0:T(8,128)(2,1)S(1)}, u32[]{:S(2)}, u32[]{:S(2)}) collective-permute-start(bf16[256,1024]{1,0:T(8,128)(2,1)S(1)} %shard_map.86.refs_2_), channel_id=1, source_target_pairs={{4,1},{6,3},{9,12},{11,14},{20,17},{22,19},{25,28},{27,30}} | collective-permute-start | bytes 1572872 | tf_op jit(solution)/shard_map/ppermute | solution.py:476
  144.2 13.8 %collective-permute-start.23 = (bf16[1024,256]{1,0:T(8,128)(2,1)S(1)}, bf16[1024,256]{1,0:T(8,128)(2,1)S(1)}, u32[]{:S(2)}, u32[]{:S(2)}) collective-permute-start(bf16[1024,256]{1,0:T(8,128)(2,1)S(1)} %get-tuple-element.34), channel_id=1, source_target_pairs={{0,2},{2,0},{5,7},{7,5},{10,8},{8,10},{15,13},{13,15},{16,18},{18,... | collective-permute-start | bytes 1572872 | tf_op jit(solution)/shard_map/ppermute | solution.py:440
  151.3 11.1 %collective-permute-start.11 = (bf16[256,1024]{1,0:T(8,128)(2,1)S(1)}, bf16[256,1024]{1,0:T(8,128)(2,1)S(1)}, u32[]{:S(2)}, u32[]{:S(2)}) collective-permute-start(bf16[256,1024]{1,0:T(8,128)(2,1)S(1)} %shard_map.86.refs_2_), channel_id=1, source_target_pairs={{5,1},{7,3},{8,12},{10,14},{21,17},{23,19},{24,28},{26,30}} | collective-permute-start | bytes 1572872 | tf_op jit(solution)/shard_map/ppermute | solution.py:476
  153.9 14.6 %collective-permute-start.30 = (bf16[1024,256]{1,0:T(8,128)(2,1)S(1)}, bf16[1024,256]{1,0:T(8,128)(2,1)S(1)}, u32[]{:S(2)}, u32[]{:S(2)}) collective-permute-start(bf16[1024,256]{1,0:T(8,128)(2,1)S(1)} %shard_map.99.refs_0_.end_a), channel_id=1, source_target_pairs={{1,3},{14,12},{17,19},{30,28}} | collective-permute-start | bytes 1572872 | tf_op jit(solution)/shard_map/ppermute | solution.py:440
  156.8 11.0 %collective-permute-start.34 = (bf16[512,256]{1,0:T(8,128)(2,1)S(1)}, bf16[512,256]{1,0:T(8,128)(2,1)S(1)}, u32[]{:S(2)}, u32[]{:S(2)}) collective-permute-start(bf16[512,256]{1,0:T(8,128)(2,1)S(1)} %get-tuple-element.37.end_b), channel_id=1, source_target_pairs={{1,3},{14,12},{17,19},{30,28}} | collective-permute-start | bytes 786440 | tf_op jit(solution)/shard_map/ppermute | solution.py:440
  158.1 24.4 %collective-permute-start.27 = (bf16[512,768]{1,0:T(8,128)(2,1)S(1)}, bf16[512,768]{1,0:T(8,128)(2,1)S(1)}, u32[]{:S(2)}, u32[]{:S(2)}) collective-permute-start(bf16[512,768]{1,0:T(8,128)(2,1)S(1)} %shard_map.98), channel_id=1, source_target_pairs={{1,17},{4,20},{6,22},{9,25},{11,27},{14,30},{17,1},{20,4},{22,6},{... | collective-permute-start | bytes 2359304 | tf_op jit(solution)/shard_map/ppermute | solution.py:610
  158.8 13.9 %collective-permute-start.36 = (bf16[512,256]{1,0:T(8,128)(2,1)S(1)}, bf16[512,256]{1,0:T(8,128)(2,1)S(1)}, u32[]{:S(2)}, u32[]{:S(2)}) collective-permute-start(bf16[512,256]{1,0:T(8,128)(2,1)S(1)} %get-tuple-element.38), channel_id=1, source_target_pairs={{3,19},{12,28},{19,3},{28,12}} | collective-permute-start | bytes 786440 | tf_op jit(solution)/shard_map/ppermute | solution.py:610
  162.4 14.0 %collective-permute-start.35 = (bf16[512,256]{1,0:T(8,128)(2,1)S(1)}, bf16[512,256]{1,0:T(8,128)(2,1)S(1)}, u32[]{:S(2)}, u32[]{:S(2)}) collective-permute-start(bf16[512,256]{1,0:T(8,128)(2,1)S(1)} %get-tuple-element.38), channel_id=1, source_target_pairs={{1,19},{14,28},{17,3},{30,12}} | collective-permute-start | bytes 786440 | tf_op jit(solution)/shard_map/ppermute | solution.py:610
  167.8 14.6 %collective-permute-start.21 = (bf16[512,512]{1,0:T(8,128)(2,1)S(1)}, bf16[512,512]{1,0:T(8,128)(2,1)S(1)}, u32[]{:S(2)}, u32[]{:S(2)}) collective-permute-start(bf16[512,512]{1,0:T(8,128)(2,1)S(1)} %shard_map.92), channel_id=1, source_target_pairs={{2,18},{7,23},{8,24},{13,29},{18,2},{23,7},{24,8},{29,13}} | collective-permute-start | bytes 1572872 | tf_op jit(solution)/shard_map/ppermute | solution.py:610
  168.5 9.2 %collective-permute-start.24 = (bf16[512,256]{1,0:T(8,128)(2,1)S(1)}, bf16[512,256]{1,0:T(8,128)(2,1)S(1)}, u32[]{:S(2)}, u32[]{:S(2)}) collective-permute-start(bf16[512,256]{1,0:T(8,128)(2,1)S(1)} %shard_map.95), channel_id=1, source_target_pairs={{2,18},{7,23},{8,24},{13,29},{18,2},{23,7},{24,8},{29,13}} | collective-permute-start | bytes 786440 | tf_op jit(solution)/shard_map/ppermute | solution.py:610
  176.4 8.5 %collective-permute-start.13 = (bf16[512,256]{1,0:T(8,128)(2,1)S(1)}, bf16[512,256]{1,0:T(8,128)(2,1)S(1)}, u32[]{:S(2)}, u32[]{:S(2)}) collective-permute-start(bf16[512,256]{1,0:T(8,128)(2,1)S(1)} %get-tuple-element.26.kept), channel_id=1, source_target_pairs={{1,3},{14,12},{17,19},{30,28}} | collective-permute-start | bytes 786440 | tf_op jit(solution)/shard_map/ppermute | solution.py:440
  181.2 9.2 %collective-permute-start.14 = (bf16[512,256]{1,0:T(8,128)(2,1)S(1)}, bf16[512,256]{1,0:T(8,128)(2,1)S(1)}, u32[]{:S(2)}, u32[]{:S(2)}) collective-permute-start(bf16[512,256]{1,0:T(8,128)(2,1)S(1)} %get-tuple-element.27), channel_id=1, source_target_pairs={{1,19},{14,28},{17,3},{30,12}} | collective-permute-start | bytes 786440 | tf_op jit(solution)/shard_map/ppermute | solution.py:610
  (14 other events, 115.5 us)

commit v2 on v1

--- a/solution.py
+++ b/solution.py
@@ -279,14 +279,14 @@
         copy.wait()
 
 
-def cut_kernel(where, weight, low_a, low_b, high, sems):
-    rows, first = high.shape[0], low_a.shape[0]
-    start = where[1] * rows
-
-    def part(at, ref):
-        return weight.at[pl.ds(pl.multiple_of(start + at, 128), ref.shape[0])], ref
-
-    run(sems, part(0, low_a), part(0, high), part(first, low_b))
+def cut_kernel(where, weight, *refs, half):
+    outs, sems = refs[:-1], refs[-1]
+    at, pairs = 0, []
+    for out in outs:
+        start = pl.multiple_of(where[1] * half + at, 128)
+        pairs.append((weight.at[pl.ds(start, out.shape[0])], out))
+        at += out.shape[0]
+    run(sems, *pairs)
 
 
 def pick_kernel(where, low, high, *refs, upper, start):
@@ -445,15 +445,19 @@
 
     up = [(i, i + 1) for i in range(count - 1)]
     down = [(i + 1, i) for i in range(count - 1)]
-    low_a, low_b, mine = pl.pallas_call(
-        cut_kernel,
-        in_specs=[SMEM, HBM],
-        out_shape=[
-            pltpu.VMEM((rows, wide), jnp.bfloat16) for rows in (2 * cut, cut, half)
-        ],
-        scratch_shapes=[pltpu.SemaphoreType.DMA((3,))],
-        compiler_params=limit(2),
-    )(where, out_weight)
+    held = pltpu.with_memory_space_constraint(out_weight, pltpu.HBM)
+
+    def take(*sizes):
+        return pl.pallas_call(
+            functools.partial(cut_kernel, half=half),
+            in_specs=[SMEM, HBM],
+            out_shape=[pltpu.VMEM((rows, wide), jnp.bfloat16) for rows in sizes],
+            scratch_shapes=[pltpu.SemaphoreType.DMA((len(sizes),))],
+            compiler_params=limit(2),
+        )(where, held)
+
+    (mine,) = take(half)
+    low_a, low_b = take(2 * cut, cut)
     low = [lax.ppermute(low_a, "seq", up), lax.ppermute(low_b, "seq", up)]
     high = lax.ppermute(mine, "seq", down)
     low2 = [lax.ppermute(low[n], "seq", up[1:]) for n in range(2)]
@@ -613,7 +617,7 @@
         return anywhere(total, [((g, b, f), (1 - g, b, f)) for g in range(2) for b, f in owners])
 
     plan = [(side * half, half, 0, side * tok_rows, 0) for side in range(2)]
-    made = product((2 * tok_rows, half), (gated,), (out_weight,), plan, HBM)
+    made = product((2 * tok_rows, half), (gated,), (held,), plan, HBM)
     own = (made, from_core(made, {b: b for b in index}))
 
     nears = [(b, f) for b in index for f in (b - 1, b + 1) if 0 <= f < count]

time: 193 us -> 205 us (1.062)
  the two profiles are of different devices: /device:TPU:28 before, /device:TPU:24 now
where the time goes in v2:
time: 205 us; the launch traced here: 204 us
  waiting for transfers between devices  108 us (53%)
  starting transfers between devices  52.7 us (26%)
  Pallas kernels  43.1 us (21%)
    ppermute x2, waiting for transfers between devices, shards_grid(): low2 = [lax.ppermute(low[n], 'seq', up[1:]) for n in range(2)]  41.1 us
    ppermute x2, waiting for transfers between devices, shards_grid(): low = [lax.ppermute(low_a, 'seq', up), lax.ppermute(low_b, 'seq', up)]  25.9 us
    ppermute x6, waiting for transfers between devices, shards_grid(): lax.ppermute(part, ('seq', 'head'), [(b * count + (h ^ turn), end * count...  20.7 us
    ppermute x12, starting transfers between devices, across(): lax.ppermute(value, ('seq', 'head'), [(b * count + h, b * count + k) for...  16.6 us
    ppermute x8, starting transfers between devices, anywhere(): return lax.ppermute(value, ('groups', 'seq', 'head'), flat)  14 us
    pallas_call x4, Pallas kernels, product(): pl.pallas_call(functools.partial(product_kernel, lefts=len(lefts), weight...  13.6 us
    ppermute x6, starting transfers between devices, shards_grid(): lax.ppermute(part, ('seq', 'head'), [(b * count + (h ^ turn), end * count...  7.74 us
    ppermute x8, waiting for transfers between devices, anywhere(): return lax.ppermute(value, ('groups', 'seq', 'head'), flat)  7.68 us
  transfers between devices with their start and end apart: 37, of which 16 were waited for; matrix products, arithmetic and copies ran while one was open for 0% of the time, Pallas kernels for 16%

profile of v2, /device:TPU:24, one launch (start us, length us, event | category | flops | bytes accessed | tf_op | source)
XLA Modules:
  0.0 204.4 jit_solution(3099474525942514210)
XLA Ops:
  0.1 2.1 %shard_map.86 = bf16[768,1024]{1,0:T(8,128)(2,1)S(1)} custom-call(s32[3]{0:T(128)S(1)} %pad_add_fusion.where, bf16[1536,1024]{1,0:T(8,128)(2,1)} %refs_1_.1), custom_call_target="tpu_custom_call" | custom-call | tf_op jit(solution)/shard_map/pallas_call | solution.py:451
  2.2 2.5 %collective-permute-start.9 = (bf16[768,1024]{1,0:T(8,128)(2,1)S(1)}, bf16[768,1024]{1,0:T(8,128)(2,1)S(1)}, u32[]{:S(2)}, u32[]{:S(2)}) collective-permute-start(bf16[768,1024]{1,0:T(8,128)(2,1)S(1)} %shard_map.86), channel_id=1, source_target_pairs={{4,0},{8,4},{12,8},{5,1},{9,5},{13,9},{6,2},{10,6},{14,10},{7,3},{... | collective-permute-start | bytes 4718600 | tf_op jit(solution)/shard_map/ppermute | solution.py:462
  4.7 2.4 %shard_map.83 = bf16[8,128,128]{2,1,0:T(8,128)(2,1)S(1)} custom-call(s32[3]{0:T(128)S(1)} %pad_add_fusion.where, s32[4]{0:T(128)S(1)} %copy-done.4, s32[8]{0:T(128)S(1)} %copy-done.5, bf16[512,1024]{1,0:T(8,128)(2,1)S(1)} %copy-done, bf16[512,1024]{1,0:T(8,128)(2,1)S(1)} %copy-done.1), custom_call_target="tpu_custom_call" | custom-call | tf_op jit(solution)/shard_map/pallas_call | solution.py:497
  9.9 1.9 shard_map.85
  13.1 5.1 %shard_map.82.intra = f32[512,1024]{1,0:T(8,128)S(1)} custom-call(s32[3]{0:T(128)S(1)} %pad_add_fusion.where, s32[4]{0:T(128)S(1)} %copy-done.4, s32[8]{0:T(128)S(1)} %copy-done.5, bf16[512,1024]{1,0:T(8,128)(2,1)S(1)} %copy-done.2, bf16[512,1024]{1,0:T(8,128)(2,1)S(1)} %copy-done, bf16[512,1024]{1,0:T(8,128)(2,1)S(1)} %copy-done.1), custom_call_target="tpu_custom_call" | custom-call | tf_op jit(solution)/shard_map/pallas_call | solution.py:507
  18.2 5.2 %collective-permute-done.1.far = bf16[8,128,128]{2,1,0:T(8,128)(2,1)S(1)} collective-permute-done((bf16[8,128,128]{2,1,0:T(8,128)(2,1)S(1)}, bf16[8,128,128]{2,1,0:T(8,128)(2,1)S(1)}, u32[]{:S(2)}, u32[]{:S(2)}) %collective-permute-start.1) | collective-permute-done | bytes 262176 | tf_op jit(solution)/shard_map/ppermute | solution.py:506
  23.4 1.8 collective-permute-done.near
  25.2 3.6 %shard_map.84 = (bf16[512,1024]{1,0:T(8,128)(2,1)S(1)}, f32[8,512]{1,0:T(8,128)S(1)}) custom-call(s32[3]{0:T(128)S(1)} %pad_add_fusion.where, s32[4]{0:T(128)S(1)} %copy-done.4, s32[8]{0:T(128)S(1)} %copy-done.5, bf16[512,1024]{1,0:T(8,128)(2,1)S(1)} %copy-done.2, f32[512,1024]{1,0:T(8,128)S(1)} %shard_map.82.intra, ...), custom_call_target="tpu_custom_call" | custom-call | tf_op jit(solution)/shard_map/pallas_call | solution.py:515
  31.6 25.9 %collective-permute-done.7.refs_3_ = bf16[256,1024]{1,0:T(8,128)(2,1)S(1)} collective-permute-done((bf16[256,1024]{1,0:T(8,128)(2,1)S(1)}, bf16[256,1024]{1,0:T(8,128)(2,1)S(1)}, u32[]{:S(2)}, u32[]{:S(2)}) %collective-permute-start.7) | collective-permute-done | bytes 524320 | tf_op jit(solution)/shard_map/ppermute | solution.py:461
  57.5 5.8 %shard_map.97.made = bf16[1024,1536]{1,0:T(8,128)(2,1)S(1)} custom-call(bf16[512,1024]{1,0:T(8,128)(2,1)S(1)} %get-tuple-element.22.own.refs_0_, bf16[512,1024]{1,0:T(8,128)(2,1)S(1)} %collective-permute-done.4.other.refs_1_, bf16[512,1024]{1,0:T(8,128)(2,1)S(1)} %collective-permute-done.17.refs_2_, bf16[256,1024]{1,0:T(8,128)(2,1)S(1)} %collective-permute-done.7.refs_3_, ...), custom_call_target="tpu_custom_call" | custom-call | flops 3221225472 | bytes 8388608 | tf_op jit(solution)/shard_map/pallas_call | solution.py:541
  66.6 5.4 %shard_map.89.own = bf16[1024,768]{1,0:T(8,128)(2,1)S(1)} custom-call(bf16[512,1024]{1,0:T(8,128)(2,1)S(1)} %get-tuple-element.22.own.refs_0_, bf16[1536,1024]{1,0:T(8,128)(2,1)} %refs_1_.1), custom_call_target="tpu_custom_call" | custom-call | flops 1610612736 | bytes 8388608 | tf_op jit(solution)/shard_map/pallas_call | solution.py:541
  72.1 3.3 %collective-permute-start.16 = (bf16[1024,768]{1,0:T(8,128)(2,1)S(1)}, bf16[1024,768]{1,0:T(8,128)(2,1)S(1)}, u32[]{:S(2)}, u32[]{:S(2)}) collective-permute-start(bf16[1024,768]{1,0:T(8,128)(2,1)S(1)} %shard_map.89.own), channel_id=1, source_target_pairs={{1,0},{3,2},{4,5},{6,7},{9,8},{11,10},{12,13},{14,15},{17,16},{19,... | collective-permute-start | bytes 4718600 | tf_op jit(solution)/shard_map/ppermute | solution.py:440
  75.5 22.6 %collective-permute-done.18.low = bf16[512,1024]{1,0:T(8,128)(2,1)S(1)} collective-permute-done((bf16[512,1024]{1,0:T(8,128)(2,1)S(1)}, bf16[512,1024]{1,0:T(8,128)(2,1)S(1)}, u32[]{:S(2)}, u32[]{:S(2)}) %collective-permute-start.18) | collective-permute-done | bytes 1048608 | tf_op jit(solution)/shard_map/ppermute | solution.py:463
  98.7 1.6 shard_map.91.two
  100.3 1.8 collective-permute-start.19
  102.2 2.1 %collective-permute-done.2 = f32[8,512]{1,0:T(8,128)S(1)} collective-permute-done((f32[8,512]{1,0:T(8,128)S(1)}, f32[8,512]{1,0:T(8,128)S(1)}, u32[]{:S(2)}, u32[]{:S(2)}) %collective-permute-start.2) | collective-permute-done | bytes 16416 | tf_op jit(solution)/shard_map/ppermute | solution.py:535
  105.8 2.3 %collective-permute-done.3.squares_more = f32[8,512]{1,0:T(8,128)S(1)} collective-permute-done((f32[8,512]{1,0:T(8,128)S(1)}, f32[8,512]{1,0:T(8,128)S(1)}, u32[]{:S(2)}, u32[]{:S(2)}) %collective-permute-start.3) | collective-permute-done | bytes 16416 | tf_op jit(solution)/shard_map/ppermute | solution.py:536
  109.6 2.2 %shard_map.98 = (bf16[1024,768]{1,0:T(8,128)(2,1)S(1)}, bf16[1024,768]{1,0:T(8,128)(2,1)S(1)}) custom-call(s32[3]{0:T(128)S(1)} %pad_add_fusion.where, bf16[1024,1536]{1,0:T(8,128)(2,1)S(1)} %shard_map.97.made, bf16[1024,1536]{1,0:T(8,128)(2,1)S(1)} %collective-permute-done.25.come), custom_call_target="tpu_custom_call" | custom-call | flops 1572864 | bytes 9437184 | tf_op jit(solution)/shard_map/pallas_call | solution.py:565
  111.9 18.5 %collective-permute-done.8.low = bf16[256,1024]{1,0:T(8,128)(2,1)S(1)} collective-permute-done((bf16[256,1024]{1,0:T(8,128)(2,1)S(1)}, bf16[256,1024]{1,0:T(8,128)(2,1)S(1)}, u32[]{:S(2)}, u32[]{:S(2)}) %collective-permute-start.8) | collective-permute-done | bytes 524320 | tf_op jit(solution)/shard_map/ppermute | solution.py:463
  130.4 3.5 %collective-permute-start.26 = (bf16[1024,768]{1,0:T(8,128)(2,1)S(1)}, bf16[1024,768]{1,0:T(8,128)(2,1)S(1)}, u32[]{:S(2)}, u32[]{:S(2)}) collective-permute-start(bf16[1024,768]{1,0:T(8,128)(2,1)S(1)} %get-tuple-element.34), channel_id=1, source_target_pairs={{3,1},{6,4},{4,6},{11,9},{9,11},{12,14},{19,17},{22,20},{20,22},{2... | collective-permute-start | bytes 4718600 | tf_op jit(solution)/shard_map/ppermute | solution.py:440
  137.8 1.6 shard_map.92
  140.7 7.4 %collective-permute-done.29.weight_turned = bf16[256,1024]{1,0:T(8,128)(2,1)S(1)} collective-permute-done((bf16[256,1024]{1,0:T(8,128)(2,1)S(1)}, bf16[256,1024]{1,0:T(8,128)(2,1)S(1)}, u32[]{:S(2)}, u32[]{:S(2)}) %collective-permute-start.29) | collective-permute-done | bytes 524320 | tf_op jit(solution)/shard_map/ppermute | solution.py:480
  150.2 1.6 collective-permute-done.28.weight
  153.2 6.1 %collective-permute-done.33.weight_turned = bf16[256,1024]{1,0:T(8,128)(2,1)S(1)} collective-permute-done((bf16[256,1024]{1,0:T(8,128)(2,1)S(1)}, bf16[256,1024]{1,0:T(8,128)(2,1)S(1)}, u32[]{:S(2)}, u32[]{:S(2)}) %collective-permute-start.33) | collective-permute-done | bytes 524320 | tf_op jit(solution)/shard_map/ppermute | solution.py:480
  165.4 5.5 %collective-permute-done.12.weight_turned = bf16[256,1024]{1,0:T(8,128)(2,1)S(1)} collective-permute-done((bf16[256,1024]{1,0:T(8,128)(2,1)S(1)}, bf16[256,1024]{1,0:T(8,128)(2,1)S(1)}, u32[]{:S(2)}, u32[]{:S(2)}) %collective-permute-start.12) | collective-permute-done | bytes 524320 | tf_op jit(solution)/shard_map/ppermute | solution.py:480
  175.2 3.4 %collective-permute-start.36 = (bf16[512,256]{1,0:T(8,128)(2,1)S(1)}, bf16[512,256]{1,0:T(8,128)(2,1)S(1)}, u32[]{:S(2)}, u32[]{:S(2)}) collective-permute-start(bf16[512,256]{1,0:T(8,128)(2,1)S(1)} %get-tuple-element.36), channel_id=1, source_target_pairs={{3,19},{12,28},{19,3},{28,12}} | collective-permute-start | bytes 786440 | tf_op jit(solution)/shard_map/ppermute | solution.py:614
  181.2 3.4 %collective-permute-start.31 = (bf16[512,256]{1,0:T(8,128)(2,1)S(1)}, bf16[512,256]{1,0:T(8,128)(2,1)S(1)}, u32[]{:S(2)}, u32[]{:S(2)}) collective-permute-start(bf16[512,256]{1,0:T(8,128)(2,1)S(1)} %shard_map.101), channel_id=1, source_target_pairs={{3,19},{12,28},{19,3},{28,12}} | collective-permute-start | bytes 786440 | tf_op jit(solution)/shard_map/ppermute | solution.py:614
  190.9 2.5 %collective-permute-start.15 = (bf16[512,256]{1,0:T(8,128)(2,1)S(1)}, bf16[512,256]{1,0:T(8,128)(2,1)S(1)}, u32[]{:S(2)}, u32[]{:S(2)}) collective-permute-start(bf16[512,256]{1,0:T(8,128)(2,1)S(1)} %get-tuple-element.25), channel_id=1, source_target_pairs={{3,19},{12,28},{19,3},{28,12}} | collective-permute-start | bytes 786440 | tf_op jit(solution)/shard_map/ppermute | solution.py:614
  194.7 2.4 %shard_map.103.most = bf16[512,1536]{1,0:T(8,128)(2,1)} custom-call(s32[3]{0:T(128)S(1)} %pad_add_fusion.where, f32[8,512]{1,0:T(8,128)S(1)} %add.3.squares, f32[8,512]{1,0:T(8,128)S(1)} %collective-permute-done.3.squares_more, bf16[1024,512]{1,0:T(8,128)(2,1)S(1)} %get-tuple-element.29.refs_0_.kept_a, ...), custom_call_target="tpu_custom_call" | custom-call | tf_op jit(solution)/shard_map/pallas_call | solution.py:658
  197.1 2.1 %collective-permute-done.15.back = bf16[512,256]{1,0:T(8,128)(2,1)S(1)} collective-permute-done((bf16[512,256]{1,0:T(8,128)(2,1)S(1)}, bf16[512,256]{1,0:T(8,128)(2,1)S(1)}, u32[]{:S(2)}, u32[]{:S(2)}) %collective-permute-start.15) | collective-permute-done | bytes 262176 | tf_op jit(solution)/shard_map/ppermute | solution.py:614
  199.2 3.4 %collective-permute-done.14.across = bf16[512,256]{1,0:T(8,128)(2,1)S(1)} collective-permute-done((bf16[512,256]{1,0:T(8,128)(2,1)S(1)}, bf16[512,256]{1,0:T(8,128)(2,1)S(1)}, u32[]{:S(2)}, u32[]{:S(2)}) %collective-permute-start.14) | collective-permute-done | bytes 262176 | tf_op jit(solution)/shard_map/ppermute | solution.py:614
  202.6 1.6 shard_map.104
  (82 shorter events, 43.1 us)
Async XLA Ops:
  2.2 55.3 %collective-permute-start.9 = (bf16[768,1024]{1,0:T(8,128)(2,1)S(1)}, bf16[768,1024]{1,0:T(8,128)(2,1)S(1)}, u32[]{:S(2)}, u32[]{:S(2)}) collective-permute-start(bf16[768,1024]{1,0:T(8,128)(2,1)S(1)} %shard_map.86), channel_id=1, source_target_pairs={{4,0},{8,4},{12,8},{5,1},{9,5},{13,9},{6,2},{10,6},{14,10},{7,3},{... | collective-permute-start | bytes 4718600 | tf_op jit(solution)/shard_map/ppermute | solution.py:462
  7.1 16.2 %collective-permute-start.1 = (bf16[8,128,128]{2,1,0:T(8,128)(2,1)S(1)}, bf16[8,128,128]{2,1,0:T(8,128)(2,1)S(1)}, u32[]{:S(2)}, u32[]{:S(2)}) collective-permute-start(bf16[8,128,128]{2,1,0:T(8,128)(2,1)S(1)} %shard_map.83), channel_id=1, source_target_pairs={{0,8},{4,12},{1,9},{5,13},{2,10},{6,14},{3,11},{7,15},{16,24},{20,... | collective-permute-start | bytes 786440 | tf_op jit(solution)/shard_map/ppermute | solution.py:506
  8.6 16.6 %collective-permute-start = (bf16[8,128,128]{2,1,0:T(8,128)(2,1)S(1)}, bf16[8,128,128]{2,1,0:T(8,128)(2,1)S(1)}, u32[]{:S(2)}, u32[]{:S(2)}) collective-permute-start(bf16[8,128,128]{2,1,0:T(8,128)(2,1)S(1)} %shard_map.83), channel_id=1, source_target_pairs={{0,4},{4,8},{8,12},{1,5},{5,9},{9,13},{2,6},{6,10},{10,14},{3,7},{... | collective-permute-start | bytes 786440 | tf_op jit(solution)/shard_map/ppermute | solution.py:505
  11.8 45.7 %collective-permute-start.17 = (bf16[512,1024]{1,0:T(8,128)(2,1)S(1)}, bf16[512,1024]{1,0:T(8,128)(2,1)S(1)}, u32[]{:S(2)}, u32[]{:S(2)}) collective-permute-start(bf16[512,1024]{1,0:T(8,128)(2,1)S(1)} %get-tuple-element.26), channel_id=1, source_target_pairs={{0,4},{4,8},{8,12},{1,5},{5,9},{9,13},{2,6},{6,10},{10,14},{3,7},{... | collective-permute-start | bytes 3145736 | tf_op jit(solution)/shard_map/ppermute | solution.py:461
  28.7 28.8 %collective-permute-start.4 = (bf16[512,1024]{1,0:T(8,128)(2,1)S(1)}, bf16[512,1024]{1,0:T(8,128)(2,1)S(1)}, u32[]{:S(2)}, u32[]{:S(2)}) collective-permute-start(bf16[512,1024]{1,0:T(8,128)(2,1)S(1)} %get-tuple-element.22.own.refs_0_), channel_id=1, source_target_pairs={{0,16},{16,0},{1,17},{17,1},{2,18},{18,2},{3,19},{19,3},{4,20},{20... | collective-permute-start | bytes 3145736 | tf_op jit(solution)/shard_map/ppermute | solution.py:530
  30.3 27.2 %collective-permute-start.7 = (bf16[256,1024]{1,0:T(8,128)(2,1)S(1)}, bf16[256,1024]{1,0:T(8,128)(2,1)S(1)}, u32[]{:S(2)}, u32[]{:S(2)}) collective-permute-start(bf16[256,1024]{1,0:T(8,128)(2,1)S(1)} %get-tuple-element.23), channel_id=1, source_target_pairs={{0,4},{4,8},{8,12},{1,5},{5,9},{9,13},{2,6},{6,10},{10,14},{3,7},{... | collective-permute-start | bytes 1572872 | tf_op jit(solution)/shard_map/ppermute | solution.py:461
  63.3 46.3 %collective-permute-start.25 = (bf16[1024,1536]{1,0:T(8,128)(2,1)S(1)}, bf16[1024,1536]{1,0:T(8,128)(2,1)S(1)}, u32[]{:S(2)}, u32[]{:S(2)}) collective-permute-start(bf16[1024,1536]{1,0:T(8,128)(2,1)S(1)} %shard_map.97.made), channel_id=1, source_target_pairs={{0,1},{2,3},{5,4},{7,6},{8,9},{10,11},{13,12},{15,14},{16,17},{18,... | collective-permute-start | bytes 9437192 | tf_op jit(solution)/shard_map/ppermute | solution.py:440
  64.6 33.5 %collective-permute-start.10 = (bf16[768,1024]{1,0:T(8,128)(2,1)S(1)}, bf16[768,1024]{1,0:T(8,128)(2,1)S(1)}, u32[]{:S(2)}, u32[]{:S(2)}) collective-permute-start(bf16[768,1024]{1,0:T(8,128)(2,1)S(1)} %collective-permute-done.9.refs_4_), channel_id=1, source_target_pairs={{4,0},{8,4},{5,1},{9,5},{6,2},{10,6},{7,3},{11,7},{20,16},{24,20},... | collective-permute-start | bytes 4718600 | tf_op jit(solution)/shard_map/ppermute | solution.py:464
  65.3 32.7 %collective-permute-start.18 = (bf16[512,1024]{1,0:T(8,128)(2,1)S(1)}, bf16[512,1024]{1,0:T(8,128)(2,1)S(1)}, u32[]{:S(2)}, u32[]{:S(2)}) collective-permute-start(bf16[512,1024]{1,0:T(8,128)(2,1)S(1)} %collective-permute-done.17.refs_2_), channel_id=1, source_target_pairs={{4,8},{8,12},{5,9},{9,13},{6,10},{10,14},{7,11},{11,15},{20,24},{2... | collective-permute-start | bytes 3145736 | tf_op jit(solution)/shard_map/ppermute | solution.py:463
  72.1 63.1 %collective-permute-start.16 = (bf16[1024,768]{1,0:T(8,128)(2,1)S(1)}, bf16[1024,768]{1,0:T(8,128)(2,1)S(1)}, u32[]{:S(2)}, u32[]{:S(2)}) collective-permute-start(bf16[1024,768]{1,0:T(8,128)(2,1)S(1)} %shard_map.89.own), channel_id=1, source_target_pairs={{1,0},{3,2},{4,5},{6,7},{9,8},{11,10},{12,13},{14,15},{17,16},{19,... | collective-permute-start | bytes 4718600 | tf_op jit(solution)/shard_map/ppermute | solution.py:440
  75.4 58.4 %collective-permute-start.5 = (bf16[512,1024]{1,0:T(8,128)(2,1)S(1)}, bf16[512,1024]{1,0:T(8,128)(2,1)S(1)}, u32[]{:S(2)}, u32[]{:S(2)}) collective-permute-start(bf16[512,1024]{1,0:T(8,128)(2,1)S(1)} %get-tuple-element.22.own.refs_0_), channel_id=1, source_target_pairs={{0,1},{1,0},{2,3},{3,2},{4,5},{5,4},{6,7},{7,6},{8,9},{9,8},{10,11... | collective-permute-start | bytes 3145736 | tf_op jit(solution)/shard_map/ppermute | solution.py:440
  100.3 36.1 %collective-permute-start.19 = (bf16[1024,512]{1,0:T(8,128)(2,1)S(1)}, bf16[1024,512]{1,0:T(8,128)(2,1)S(1)}, u32[]{:S(2)}, u32[]{:S(2)}) collective-permute-start(bf16[1024,512]{1,0:T(8,128)(2,1)S(1)} %shard_map.91.two), channel_id=1, source_target_pairs={{1,0},{3,2},{4,5},{6,7},{9,8},{11,10},{12,13},{14,15},{17,16},{19,... | collective-permute-start | bytes 3145736 | tf_op jit(solution)/shard_map/ppermute | solution.py:440
  108.1 22.3 %collective-permute-start.8 = (bf16[256,1024]{1,0:T(8,128)(2,1)S(1)}, bf16[256,1024]{1,0:T(8,128)(2,1)S(1)}, u32[]{:S(2)}, u32[]{:S(2)}) collective-permute-start(bf16[256,1024]{1,0:T(8,128)(2,1)S(1)} %collective-permute-done.7.refs_3_), channel_id=1, source_target_pairs={{4,8},{8,12},{5,9},{9,13},{6,10},{10,14},{7,11},{11,15},{20,24},{2... | collective-permute-start | bytes 1572872 | tf_op jit(solution)/shard_map/ppermute | solution.py:463
  109.6 29.8 %collective-permute-start.6 = (bf16[512,1024]{1,0:T(8,128)(2,1)S(1)}, bf16[512,1024]{1,0:T(8,128)(2,1)S(1)}, u32[]{:S(2)}, u32[]{:S(2)}) collective-permute-start(bf16[512,1024]{1,0:T(8,128)(2,1)S(1)} %collective-permute-done.4.other.refs_1_), channel_id=1, source_target_pairs={{0,1},{1,0},{2,3},{3,2},{4,5},{5,4},{6,7},{7,6},{8,9},{9,8},{10,11... | collective-permute-start | bytes 3145736 | tf_op jit(solution)/shard_map/ppermute | solution.py:440
  130.4 42.6 %collective-permute-start.26 = (bf16[1024,768]{1,0:T(8,128)(2,1)S(1)}, bf16[1024,768]{1,0:T(8,128)(2,1)S(1)}, u32[]{:S(2)}, u32[]{:S(2)}) collective-permute-start(bf16[1024,768]{1,0:T(8,128)(2,1)S(1)} %get-tuple-element.34), channel_id=1, source_target_pairs={{3,1},{6,4},{4,6},{11,9},{9,11},{12,14},{19,17},{22,20},{20,22},{2... | collective-permute-start | bytes 4718600 | tf_op jit(solution)/shard_map/ppermute | solution.py:440
  133.9 14.2 %collective-permute-start.29 = (bf16[256,1024]{1,0:T(8,128)(2,1)S(1)}, bf16[256,1024]{1,0:T(8,128)(2,1)S(1)}, u32[]{:S(2)}, u32[]{:S(2)}) collective-permute-start(bf16[256,1024]{1,0:T(8,128)(2,1)S(1)} %get-tuple-element.27.refs_2_), channel_id=1, source_target_pairs={{4,1},{6,3},{9,12},{11,14},{20,17},{22,19},{25,28},{27,30}} | collective-permute-start | bytes 1572872 | tf_op jit(solution)/shard_map/ppermute | solution.py:480
  135.2 16.7 %collective-permute-start.28 = (bf16[256,1024]{1,0:T(8,128)(2,1)S(1)}, bf16[256,1024]{1,0:T(8,128)(2,1)S(1)}, u32[]{:S(2)}, u32[]{:S(2)}) collective-permute-start(bf16[256,1024]{1,0:T(8,128)(2,1)S(1)} %get-tuple-element.27.refs_2_), channel_id=1, source_target_pairs={{5,1},{7,3},{8,12},{10,14},{21,17},{23,19},{24,28},{26,30}} | collective-permute-start | bytes 1572872 | tf_op jit(solution)/shard_map/ppermute | solution.py:480
  136.5 22.8 %collective-permute-start.33 = (bf16[256,1024]{1,0:T(8,128)(2,1)S(1)}, bf16[256,1024]{1,0:T(8,128)(2,1)S(1)}, u32[]{:S(2)}, u32[]{:S(2)}) collective-permute-start(bf16[256,1024]{1,0:T(8,128)(2,1)S(1)} %get-tuple-element.28.refs_3_), channel_id=1, source_target_pairs={{4,1},{6,3},{9,12},{11,14},{20,17},{22,19},{25,28},{27,30}} | collective-permute-start | bytes 1572872 | tf_op jit(solution)/shard_map/ppermute | solution.py:480
  139.4 22.5 %collective-permute-start.32 = (bf16[256,1024]{1,0:T(8,128)(2,1)S(1)}, bf16[256,1024]{1,0:T(8,128)(2,1)S(1)}, u32[]{:S(2)}, u32[]{:S(2)}) collective-permute-start(bf16[256,1024]{1,0:T(8,128)(2,1)S(1)} %get-tuple-element.28.refs_3_), channel_id=1, source_target_pairs={{5,1},{7,3},{8,12},{10,14},{21,17},{23,19},{24,28},{26,30}} | collective-permute-start | bytes 1572872 | tf_op jit(solution)/shard_map/ppermute | solution.py:480
  148.1 27.1 %collective-permute-start.20 = (bf16[1024,512]{1,0:T(8,128)(2,1)S(1)}, bf16[1024,512]{1,0:T(8,128)(2,1)S(1)}, u32[]{:S(2)}, u32[]{:S(2)}) collective-permute-start(bf16[1024,512]{1,0:T(8,128)(2,1)S(1)} %get-tuple-element.30), channel_id=1, source_target_pairs={{0,2},{2,0},{5,7},{7,5},{10,8},{8,10},{15,13},{13,15},{16,18},{18,... | collective-permute-start | bytes 3145736 | tf_op jit(solution)/shard_map/ppermute | solution.py:440
  151.9 11.4 %collective-permute-start.22 = (bf16[1024,256]{1,0:T(8,128)(2,1)S(1)}, bf16[1024,256]{1,0:T(8,128)(2,1)S(1)}, u32[]{:S(2)}, u32[]{:S(2)}) collective-permute-start(bf16[1024,256]{1,0:T(8,128)(2,1)S(1)} %shard_map.94.two), channel_id=1, source_target_pairs={{1,0},{3,2},{4,5},{6,7},{9,8},{11,10},{12,13},{14,15},{17,16},{19,... | collective-permute-start | bytes 1572872 | tf_op jit(solution)/shard_map/ppermute | solution.py:440
  159.3 11.6 %collective-permute-start.12 = (bf16[256,1024]{1,0:T(8,128)(2,1)S(1)}, bf16[256,1024]{1,0:T(8,128)(2,1)S(1)}, u32[]{:S(2)}, u32[]{:S(2)}) collective-permute-start(bf16[256,1024]{1,0:T(8,128)(2,1)S(1)} %shard_map.87.refs_2_), channel_id=1, source_target_pairs={{4,1},{6,3},{9,12},{11,14},{20,17},{22,19},{25,28},{27,30}} | collective-permute-start | bytes 1572872 | tf_op jit(solution)/shard_map/ppermute | solution.py:480
  161.9 12.6 %collective-permute-start.30 = (bf16[1024,256]{1,0:T(8,128)(2,1)S(1)}, bf16[1024,256]{1,0:T(8,128)(2,1)S(1)}, u32[]{:S(2)}, u32[]{:S(2)}) collective-permute-start(bf16[1024,256]{1,0:T(8,128)(2,1)S(1)} %shard_map.100.refs_0_.end_a), channel_id=1, source_target_pairs={{1,3},{14,12},{17,19},{30,28}} | collective-permute-start | bytes 1572872 | tf_op jit(solution)/shard_map/ppermute | solution.py:440
  163.2 15.7 %collective-permute-start.11 = (bf16[256,1024]{1,0:T(8,128)(2,1)S(1)}, bf16[256,1024]{1,0:T(8,128)(2,1)S(1)}, u32[]{:S(2)}, u32[]{:S(2)}) collective-permute-start(bf16[256,1024]{1,0:T(8,128)(2,1)S(1)} %shard_map.87.refs_2_), channel_id=1, source_target_pairs={{5,1},{7,3},{8,12},{10,14},{21,17},{23,19},{24,28},{26,30}} | collective-permute-start | bytes 1572872 | tf_op jit(solution)/shard_map/ppermute | solution.py:480
  170.9 13.7 %collective-permute-start.23 = (bf16[1024,256]{1,0:T(8,128)(2,1)S(1)}, bf16[1024,256]{1,0:T(8,128)(2,1)S(1)}, u32[]{:S(2)}, u32[]{:S(2)}) collective-permute-start(bf16[1024,256]{1,0:T(8,128)(2,1)S(1)} %get-tuple-element.32), channel_id=1, source_target_pairs={{0,2},{2,0},{5,7},{7,5},{10,8},{8,10},{15,13},{13,15},{16,18},{18,... | collective-permute-start | bytes 1572872 | tf_op jit(solution)/shard_map/ppermute | solution.py:440
  174.5 20.2 %collective-permute-start.27 = (bf16[512,768]{1,0:T(8,128)(2,1)S(1)}, bf16[512,768]{1,0:T(8,128)(2,1)S(1)}, u32[]{:S(2)}, u32[]{:S(2)}) collective-permute-start(bf16[512,768]{1,0:T(8,128)(2,1)S(1)} %shard_map.99), channel_id=1, source_target_pairs={{1,17},{4,20},{6,22},{9,25},{11,27},{14,30},{17,1},{20,4},{22,6},{... | collective-permute-start | bytes 2359304 | tf_op jit(solution)/shard_map/ppermute | solution.py:614
  175.2 10.2 %collective-permute-start.36 = (bf16[512,256]{1,0:T(8,128)(2,1)S(1)}, bf16[512,256]{1,0:T(8,128)(2,1)S(1)}, u32[]{:S(2)}, u32[]{:S(2)}) collective-permute-start(bf16[512,256]{1,0:T(8,128)(2,1)S(1)} %get-tuple-element.36), channel_id=1, source_target_pairs={{3,19},{12,28},{19,3},{28,12}} | collective-permute-start | bytes 786440 | tf_op jit(solution)/shard_map/ppermute | solution.py:614
  178.9 9.3 %collective-permute-start.35 = (bf16[512,256]{1,0:T(8,128)(2,1)S(1)}, bf16[512,256]{1,0:T(8,128)(2,1)S(1)}, u32[]{:S(2)}, u32[]{:S(2)}) collective-permute-start(bf16[512,256]{1,0:T(8,128)(2,1)S(1)} %get-tuple-element.36), channel_id=1, source_target_pairs={{1,19},{14,28},{17,3},{30,12}} | collective-permute-start | bytes 786440 | tf_op jit(solution)/shard_map/ppermute | solution.py:614
  181.2 9.7 %collective-permute-start.31 = (bf16[512,256]{1,0:T(8,128)(2,1)S(1)}, bf16[512,256]{1,0:T(8,128)(2,1)S(1)}, u32[]{:S(2)}, u32[]{:S(2)}) collective-permute-start(bf16[512,256]{1,0:T(8,128)(2,1)S(1)} %shard_map.101), channel_id=1, source_target_pairs={{3,19},{12,28},{19,3},{28,12}} | collective-permute-start | bytes 786440 | tf_op jit(solution)/shard_map/ppermute | solution.py:614
  184.6 10.1 %collective-permute-start.21 = (bf16[512,512]{1,0:T(8,128)(2,1)S(1)}, bf16[512,512]{1,0:T(8,128)(2,1)S(1)}, u32[]{:S(2)}, u32[]{:S(2)}) collective-permute-start(bf16[512,512]{1,0:T(8,128)(2,1)S(1)} %shard_map.93), channel_id=1, source_target_pairs={{2,18},{7,23},{8,24},{13,29},{18,2},{23,7},{24,8},{29,13}} | collective-permute-start | bytes 1572872 | tf_op jit(solution)/shard_map/ppermute | solution.py:614
  188.2 8.9 %collective-permute-start.13 = (bf16[512,256]{1,0:T(8,128)(2,1)S(1)}, bf16[512,256]{1,0:T(8,128)(2,1)S(1)}, u32[]{:S(2)}, u32[]{:S(2)}) collective-permute-start(bf16[512,256]{1,0:T(8,128)(2,1)S(1)} %get-tuple-element.24.kept), channel_id=1, source_target_pairs={{1,3},{14,12},{17,19},{30,28}} | collective-permute-start | bytes 786440 | tf_op jit(solution)/shard_map/ppermute | solution.py:440
  193.4 9.2 %collective-permute-start.14 = (bf16[512,256]{1,0:T(8,128)(2,1)S(1)}, bf16[512,256]{1,0:T(8,128)(2,1)S(1)}, u32[]{:S(2)}, u32[]{:S(2)}) collective-permute-start(bf16[512,256]{1,0:T(8,128)(2,1)S(1)} %get-tuple-element.25), channel_id=1, source_target_pairs={{1,19},{14,28},{17,3},{30,12}} | collective-permute-start | bytes 786440 | tf_op jit(solution)/shard_map/ppermute | solution.py:614
  (12 other events, 72.7 us)

commit v3 on v2

--- a/solution.py
+++ b/solution.py
@@ -402,14 +402,17 @@
         @pl.when(at_end(where, count) & (where[1] == group))
         def _(group=group):
             scale = scale_of(squares, squares_more, width)
-            for to, one, two in ((this, kept, more), (that, across, back)):
+            copies = []
+            for n, (to, side, one, two) in enumerate(
+                ((this, group, kept, more), (that, 1 - group, across, back))
+            ):
                 total = one[...].astype(jnp.float32) + two[...].astype(jnp.float32)
                 to[...] = (total * scale).astype(jnp.bfloat16)
-            pairs = [
-                (ref, out.at[:, pl.ds(side * half + half - cut, cut)])
-                for ref, side in ((this, group), (that, 1 - group))
-            ]
-            run(sems, *pairs)
+                columns = pl.ds(side * half + half - cut, cut)
+                copies.append(pltpu.make_async_copy(to, out.at[:, columns], sems.at[n]))
+                copies[-1].start()
+            for copy in copies:
+                copy.wait()
 
 
 def shards_grid(

time: 205 us -> 205 us (level)
  no operation moved by 1% of the time
where the time goes in v3:
time: 205 us; the launch traced here: 204 us
  waiting for transfers between devices  108 us (53%)
  starting transfers between devices  52.7 us (26%)
  Pallas kernels  43.1 us (21%)
    ppermute x2, waiting for transfers between devices, shards_grid(): low2 = [lax.ppermute(low[n], 'seq', up[1:]) for n in range(2)]  41.1 us
    ppermute x2, waiting for transfers between devices, shards_grid(): low = [lax.ppermute(low_a, 'seq', up), lax.ppermute(low_b, 'seq', up)]  25.9 us
    ppermute x6, waiting for transfers between devices, shards_grid(): lax.ppermute(part, ('seq', 'head'), [(b * count + (h ^ turn), end * count...  20.7 us
    ppermute x12, starting transfers between devices, across(): lax.ppermute(value, ('seq', 'head'), [(b * count + h, b * count + k) for...  16.6 us
    ppermute x8, starting transfers between devices, anywhere(): return lax.ppermute(value, ('groups', 'seq', 'head'), flat)  14 us
    pallas_call x4, Pallas kernels, product(): pl.pallas_call(functools.partial(product_kernel, lefts=len(lefts), weight...  13.6 us
    ppermute x6, starting transfers between devices, shards_grid(): lax.ppermute(part, ('seq', 'head'), [(b * count + (h ^ turn), end * count...  7.74 us
    ppermute x8, waiting for transfers between devices, anywhere(): return lax.ppermute(value, ('groups', 'seq', 'head'), flat)  7.68 us
  transfers between devices with their start and end apart: 37, of which 16 were waited for; matrix products, arithmetic and copies ran while one was open for 0% of the time, Pallas kernels for 16%

profile of v3, /device:TPU:24, one launch (start us, length us, event | category | flops | bytes accessed | tf_op | source)
XLA Modules:
  0.0 204.4 jit_solution(3099474525942514210)
XLA Ops:
  0.1 2.1 %shard_map.86 = bf16[768,1024]{1,0:T(8,128)(2,1)S(1)} custom-call(s32[3]{0:T(128)S(1)} %pad_add_fusion.where, bf16[1536,1024]{1,0:T(8,128)(2,1)} %refs_1_.1), custom_call_target="tpu_custom_call" | custom-call | tf_op jit(solution)/shard_map/pallas_call | solution.py:454
  2.2 2.5 %collective-permute-start.9 = (bf16[768,1024]{1,0:T(8,128)(2,1)S(1)}, bf16[768,1024]{1,0:T(8,128)(2,1)S(1)}, u32[]{:S(2)}, u32[]{:S(2)}) collective-permute-start(bf16[768,1024]{1,0:T(8,128)(2,1)S(1)} %shard_map.86), channel_id=1, source_target_pairs={{4,0},{8,4},{12,8},{5,1},{9,5},{13,9},{6,2},{10,6},{14,10},{7,3},{... | collective-permute-start | bytes 4718600 | tf_op jit(solution)/shard_map/ppermute | solution.py:465
  4.7 2.4 %shard_map.83 = bf16[8,128,128]{2,1,0:T(8,128)(2,1)S(1)} custom-call(s32[3]{0:T(128)S(1)} %pad_add_fusion.where, s32[4]{0:T(128)S(1)} %copy-done.4, s32[8]{0:T(128)S(1)} %copy-done.5, bf16[512,1024]{1,0:T(8,128)(2,1)S(1)} %copy-done, bf16[512,1024]{1,0:T(8,128)(2,1)S(1)} %copy-done.1), custom_call_target="tpu_custom_call" | custom-call | tf_op jit(solution)/shard_map/pallas_call | solution.py:500
  9.9 1.9 shard_map.85
  13.1 5.1 %shard_map.82.intra = f32[512,1024]{1,0:T(8,128)S(1)} custom-call(s32[3]{0:T(128)S(1)} %pad_add_fusion.where, s32[4]{0:T(128)S(1)} %copy-done.4, s32[8]{0:T(128)S(1)} %copy-done.5, bf16[512,1024]{1,0:T(8,128)(2,1)S(1)} %copy-done.2, bf16[512,1024]{1,0:T(8,128)(2,1)S(1)} %copy-done, bf16[512,1024]{1,0:T(8,128)(2,1)S(1)} %copy-done.1), custom_call_target="tpu_custom_call" | custom-call | tf_op jit(solution)/shard_map/pallas_call | solution.py:510
  18.2 5.2 %collective-permute-done.1.far = bf16[8,128,128]{2,1,0:T(8,128)(2,1)S(1)} collective-permute-done((bf16[8,128,128]{2,1,0:T(8,128)(2,1)S(1)}, bf16[8,128,128]{2,1,0:T(8,128)(2,1)S(1)}, u32[]{:S(2)}, u32[]{:S(2)}) %collective-permute-start.1) | collective-permute-done | bytes 262176 | tf_op jit(solution)/shard_map/ppermute | solution.py:509
  23.4 1.8 collective-permute-done.near
  25.2 3.6 %shard_map.84 = (bf16[512,1024]{1,0:T(8,128)(2,1)S(1)}, f32[8,512]{1,0:T(8,128)S(1)}) custom-call(s32[3]{0:T(128)S(1)} %pad_add_fusion.where, s32[4]{0:T(128)S(1)} %copy-done.4, s32[8]{0:T(128)S(1)} %copy-done.5, bf16[512,1024]{1,0:T(8,128)(2,1)S(1)} %copy-done.2, f32[512,1024]{1,0:T(8,128)S(1)} %shard_map.82.intra, ...), custom_call_target="tpu_custom_call" | custom-call | tf_op jit(solution)/shard_map/pallas_call | solution.py:518
  31.6 25.9 %collective-permute-done.7.refs_3_ = bf16[256,1024]{1,0:T(8,128)(2,1)S(1)} collective-permute-done((bf16[256,1024]{1,0:T(8,128)(2,1)S(1)}, bf16[256,1024]{1,0:T(8,128)(2,1)S(1)}, u32[]{:S(2)}, u32[]{:S(2)}) %collective-permute-start.7) | collective-permute-done | bytes 524320 | tf_op jit(solution)/shard_map/ppermute | solution.py:464
  57.5 5.8 %shard_map.97.made = bf16[1024,1536]{1,0:T(8,128)(2,1)S(1)} custom-call(bf16[512,1024]{1,0:T(8,128)(2,1)S(1)} %get-tuple-element.22.own.refs_0_, bf16[512,1024]{1,0:T(8,128)(2,1)S(1)} %collective-permute-done.4.other.refs_1_, bf16[512,1024]{1,0:T(8,128)(2,1)S(1)} %collective-permute-done.17.refs_2_, bf16[256,1024]{1,0:T(8,128)(2,1)S(1)} %collective-permute-done.7.refs_3_, ...), custom_call_target="tpu_custom_call" | custom-call | flops 3221225472 | bytes 8388608 | tf_op jit(solution)/shard_map/pallas_call | solution.py:544
  66.6 5.4 %shard_map.89.own = bf16[1024,768]{1,0:T(8,128)(2,1)S(1)} custom-call(bf16[512,1024]{1,0:T(8,128)(2,1)S(1)} %get-tuple-element.22.own.refs_0_, bf16[1536,1024]{1,0:T(8,128)(2,1)} %refs_1_.1), custom_call_target="tpu_custom_call" | custom-call | flops 1610612736 | bytes 8388608 | tf_op jit(solution)/shard_map/pallas_call | solution.py:544
  72.1 3.3 %collective-permute-start.16 = (bf16[1024,768]{1,0:T(8,128)(2,1)S(1)}, bf16[1024,768]{1,0:T(8,128)(2,1)S(1)}, u32[]{:S(2)}, u32[]{:S(2)}) collective-permute-start(bf16[1024,768]{1,0:T(8,128)(2,1)S(1)} %shard_map.89.own), channel_id=1, source_target_pairs={{1,0},{3,2},{4,5},{6,7},{9,8},{11,10},{12,13},{14,15},{17,16},{19,... | collective-permute-start | bytes 4718600 | tf_op jit(solution)/shard_map/ppermute | solution.py:443
  75.5 22.6 %collective-permute-done.18.low = bf16[512,1024]{1,0:T(8,128)(2,1)S(1)} collective-permute-done((bf16[512,1024]{1,0:T(8,128)(2,1)S(1)}, bf16[512,1024]{1,0:T(8,128)(2,1)S(1)}, u32[]{:S(2)}, u32[]{:S(2)}) %collective-permute-start.18) | collective-permute-done | bytes 1048608 | tf_op jit(solution)/shard_map/ppermute | solution.py:466
  98.7 1.6 shard_map.91.two
  100.3 1.8 collective-permute-start.19
  102.2 2.1 %collective-permute-done.2 = f32[8,512]{1,0:T(8,128)S(1)} collective-permute-done((f32[8,512]{1,0:T(8,128)S(1)}, f32[8,512]{1,0:T(8,128)S(1)}, u32[]{:S(2)}, u32[]{:S(2)}) %collective-permute-start.2) | collective-permute-done | bytes 16416 | tf_op jit(solution)/shard_map/ppermute | solution.py:538
  105.8 2.3 %collective-permute-done.3.squares_more = f32[8,512]{1,0:T(8,128)S(1)} collective-permute-done((f32[8,512]{1,0:T(8,128)S(1)}, f32[8,512]{1,0:T(8,128)S(1)}, u32[]{:S(2)}, u32[]{:S(2)}) %collective-permute-start.3) | collective-permute-done | bytes 16416 | tf_op jit(solution)/shard_map/ppermute | solution.py:539
  109.6 2.2 %shard_map.98 = (bf16[1024,768]{1,0:T(8,128)(2,1)S(1)}, bf16[1024,768]{1,0:T(8,128)(2,1)S(1)}) custom-call(s32[3]{0:T(128)S(1)} %pad_add_fusion.where, bf16[1024,1536]{1,0:T(8,128)(2,1)S(1)} %shard_map.97.made, bf16[1024,1536]{1,0:T(8,128)(2,1)S(1)} %collective-permute-done.25.come), custom_call_target="tpu_custom_call" | custom-call | flops 1572864 | bytes 9437184 | tf_op jit(solution)/shard_map/pallas_call | solution.py:568
  111.9 18.5 %collective-permute-done.8.low = bf16[256,1024]{1,0:T(8,128)(2,1)S(1)} collective-permute-done((bf16[256,1024]{1,0:T(8,128)(2,1)S(1)}, bf16[256,1024]{1,0:T(8,128)(2,1)S(1)}, u32[]{:S(2)}, u32[]{:S(2)}) %collective-permute-start.8) | collective-permute-done | bytes 524320 | tf_op jit(solution)/shard_map/ppermute | solution.py:466
  130.4 3.5 %collective-permute-start.26 = (bf16[1024,768]{1,0:T(8,128)(2,1)S(1)}, bf16[1024,768]{1,0:T(8,128)(2,1)S(1)}, u32[]{:S(2)}, u32[]{:S(2)}) collective-permute-start(bf16[1024,768]{1,0:T(8,128)(2,1)S(1)} %get-tuple-element.34), channel_id=1, source_target_pairs={{3,1},{6,4},{4,6},{11,9},{9,11},{12,14},{19,17},{22,20},{20,22},{2... | collective-permute-start | bytes 4718600 | tf_op jit(solution)/shard_map/ppermute | solution.py:443
  137.8 1.6 shard_map.92
  140.7 7.4 %collective-permute-done.29.weight_turned = bf16[256,1024]{1,0:T(8,128)(2,1)S(1)} collective-permute-done((bf16[256,1024]{1,0:T(8,128)(2,1)S(1)}, bf16[256,1024]{1,0:T(8,128)(2,1)S(1)}, u32[]{:S(2)}, u32[]{:S(2)}) %collective-permute-start.29) | collective-permute-done | bytes 524320 | tf_op jit(solution)/shard_map/ppermute | solution.py:483
  150.2 1.6 collective-permute-done.28.weight
  153.2 6.1 %collective-permute-done.33.weight_turned = bf16[256,1024]{1,0:T(8,128)(2,1)S(1)} collective-permute-done((bf16[256,1024]{1,0:T(8,128)(2,1)S(1)}, bf16[256,1024]{1,0:T(8,128)(2,1)S(1)}, u32[]{:S(2)}, u32[]{:S(2)}) %collective-permute-start.33) | collective-permute-done | bytes 524320 | tf_op jit(solution)/shard_map/ppermute | solution.py:483
  165.4 5.5 %collective-permute-done.12.weight_turned = bf16[256,1024]{1,0:T(8,128)(2,1)S(1)} collective-permute-done((bf16[256,1024]{1,0:T(8,128)(2,1)S(1)}, bf16[256,1024]{1,0:T(8,128)(2,1)S(1)}, u32[]{:S(2)}, u32[]{:S(2)}) %collective-permute-start.12) | collective-permute-done | bytes 524320 | tf_op jit(solution)/shard_map/ppermute | solution.py:483
  175.2 3.4 %collective-permute-start.36 = (bf16[512,256]{1,0:T(8,128)(2,1)S(1)}, bf16[512,256]{1,0:T(8,128)(2,1)S(1)}, u32[]{:S(2)}, u32[]{:S(2)}) collective-permute-start(bf16[512,256]{1,0:T(8,128)(2,1)S(1)} %get-tuple-element.36), channel_id=1, source_target_pairs={{3,19},{12,28},{19,3},{28,12}} | collective-permute-start | bytes 786440 | tf_op jit(solution)/shard_map/ppermute | solution.py:617
  181.2 3.4 %collective-permute-start.31 = (bf16[512,256]{1,0:T(8,128)(2,1)S(1)}, bf16[512,256]{1,0:T(8,128)(2,1)S(1)}, u32[]{:S(2)}, u32[]{:S(2)}) collective-permute-start(bf16[512,256]{1,0:T(8,128)(2,1)S(1)} %shard_map.101), channel_id=1, source_target_pairs={{3,19},{12,28},{19,3},{28,12}} | collective-permute-start | bytes 786440 | tf_op jit(solution)/shard_map/ppermute | solution.py:617
  190.9 2.5 %collective-permute-start.15 = (bf16[512,256]{1,0:T(8,128)(2,1)S(1)}, bf16[512,256]{1,0:T(8,128)(2,1)S(1)}, u32[]{:S(2)}, u32[]{:S(2)}) collective-permute-start(bf16[512,256]{1,0:T(8,128)(2,1)S(1)} %get-tuple-element.25), channel_id=1, source_target_pairs={{3,19},{12,28},{19,3},{28,12}} | collective-permute-start | bytes 786440 | tf_op jit(solution)/shard_map/ppermute | solution.py:617
  194.7 2.4 %shard_map.103.most = bf16[512,1536]{1,0:T(8,128)(2,1)} custom-call(s32[3]{0:T(128)S(1)} %pad_add_fusion.where, f32[8,512]{1,0:T(8,128)S(1)} %add.3.squares, f32[8,512]{1,0:T(8,128)S(1)} %collective-permute-done.3.squares_more, bf16[1024,512]{1,0:T(8,128)(2,1)S(1)} %get-tuple-element.29.refs_0_.kept_a, ...), custom_call_target="tpu_custom_call" | custom-call | tf_op jit(solution)/shard_map/pallas_call | solution.py:661
  197.1 2.1 %collective-permute-done.15.back = bf16[512,256]{1,0:T(8,128)(2,1)S(1)} collective-permute-done((bf16[512,256]{1,0:T(8,128)(2,1)S(1)}, bf16[512,256]{1,0:T(8,128)(2,1)S(1)}, u32[]{:S(2)}, u32[]{:S(2)}) %collective-permute-start.15) | collective-permute-done | bytes 262176 | tf_op jit(solution)/shard_map/ppermute | solution.py:617
  199.2 3.4 %collective-permute-done.14.across = bf16[512,256]{1,0:T(8,128)(2,1)S(1)} collective-permute-done((bf16[512,256]{1,0:T(8,128)(2,1)S(1)}, bf16[512,256]{1,0:T(8,128)(2,1)S(1)}, u32[]{:S(2)}, u32[]{:S(2)}) %collective-permute-start.14) | collective-permute-done | bytes 262176 | tf_op jit(solution)/shard_map/ppermute | solution.py:617
  202.6 1.6 shard_map.104
  (82 shorter events, 43.1 us)
Async XLA Ops:
  2.2 55.3 %collective-permute-start.9 = (bf16[768,1024]{1,0:T(8,128)(2,1)S(1)}, bf16[768,1024]{1,0:T(8,128)(2,1)S(1)}, u32[]{:S(2)}, u32[]{:S(2)}) collective-permute-start(bf16[768,1024]{1,0:T(8,128)(2,1)S(1)} %shard_map.86), channel_id=1, source_target_pairs={{4,0},{8,4},{12,8},{5,1},{9,5},{13,9},{6,2},{10,6},{14,10},{7,3},{... | collective-permute-start | bytes 4718600 | tf_op jit(solution)/shard_map/ppermute | solution.py:465
  7.1 16.2 %collective-permute-start.1 = (bf16[8,128,128]{2,1,0:T(8,128)(2,1)S(1)}, bf16[8,128,128]{2,1,0:T(8,128)(2,1)S(1)}, u32[]{:S(2)}, u32[]{:S(2)}) collective-permute-start(bf16[8,128,128]{2,1,0:T(8,128)(2,1)S(1)} %shard_map.83), channel_id=1, source_target_pairs={{0,8},{4,12},{1,9},{5,13},{2,10},{6,14},{3,11},{7,15},{16,24},{20,... | collective-permute-start | bytes 786440 | tf_op jit(solution)/shard_map/ppermute | solution.py:509
  8.6 16.6 %collective-permute-start = (bf16[8,128,128]{2,1,0:T(8,128)(2,1)S(1)}, bf16[8,128,128]{2,1,0:T(8,128)(2,1)S(1)}, u32[]{:S(2)}, u32[]{:S(2)}) collective-permute-start(bf16[8,128,128]{2,1,0:T(8,128)(2,1)S(1)} %shard_map.83), channel_id=1, source_target_pairs={{0,4},{4,8},{8,12},{1,5},{5,9},{9,13},{2,6},{6,10},{10,14},{3,7},{... | collective-permute-start | bytes 786440 | tf_op jit(solution)/shard_map/ppermute | solution.py:508
  11.8 45.7 %collective-permute-start.17 = (bf16[512,1024]{1,0:T(8,128)(2,1)S(1)}, bf16[512,1024]{1,0:T(8,128)(2,1)S(1)}, u32[]{:S(2)}, u32[]{:S(2)}) collective-permute-start(bf16[512,1024]{1,0:T(8,128)(2,1)S(1)} %get-tuple-element.26), channel_id=1, source_target_pairs={{0,4},{4,8},{8,12},{1,5},{5,9},{9,13},{2,6},{6,10},{10,14},{3,7},{... | collective-permute-start | bytes 3145736 | tf_op jit(solution)/shard_map/ppermute | solution.py:464
  28.7 28.8 %collective-permute-start.4 = (bf16[512,1024]{1,0:T(8,128)(2,1)S(1)}, bf16[512,1024]{1,0:T(8,128)(2,1)S(1)}, u32[]{:S(2)}, u32[]{:S(2)}) collective-permute-start(bf16[512,1024]{1,0:T(8,128)(2,1)S(1)} %get-tuple-element.22.own.refs_0_), channel_id=1, source_target_pairs={{0,16},{16,0},{1,17},{17,1},{2,18},{18,2},{3,19},{19,3},{4,20},{20... | collective-permute-start | bytes 3145736 | tf_op jit(solution)/shard_map/ppermute | solution.py:533
  30.3 27.2 %collective-permute-start.7 = (bf16[256,1024]{1,0:T(8,128)(2,1)S(1)}, bf16[256,1024]{1,0:T(8,128)(2,1)S(1)}, u32[]{:S(2)}, u32[]{:S(2)}) collective-permute-start(bf16[256,1024]{1,0:T(8,128)(2,1)S(1)} %get-tuple-element.23), channel_id=1, source_target_pairs={{0,4},{4,8},{8,12},{1,5},{5,9},{9,13},{2,6},{6,10},{10,14},{3,7},{... | collective-permute-start | bytes 1572872 | tf_op jit(solution)/shard_map/ppermute | solution.py:464
  63.3 46.3 %collective-permute-start.25 = (bf16[1024,1536]{1,0:T(8,128)(2,1)S(1)}, bf16[1024,1536]{1,0:T(8,128)(2,1)S(1)}, u32[]{:S(2)}, u32[]{:S(2)}) collective-permute-start(bf16[1024,1536]{1,0:T(8,128)(2,1)S(1)} %shard_map.97.made), channel_id=1, source_target_pairs={{0,1},{2,3},{5,4},{7,6},{8,9},{10,11},{13,12},{15,14},{16,17},{18,... | collective-permute-start | bytes 9437192 | tf_op jit(solution)/shard_map/ppermute | solution.py:443
  64.6 33.5 %collective-permute-start.10 = (bf16[768,1024]{1,0:T(8,128)(2,1)S(1)}, bf16[768,1024]{1,0:T(8,128)(2,1)S(1)}, u32[]{:S(2)}, u32[]{:S(2)}) collective-permute-start(bf16[768,1024]{1,0:T(8,128)(2,1)S(1)} %collective-permute-done.9.refs_4_), channel_id=1, source_target_pairs={{4,0},{8,4},{5,1},{9,5},{6,2},{10,6},{7,3},{11,7},{20,16},{24,20},... | collective-permute-start | bytes 4718600 | tf_op jit(solution)/shard_map/ppermute | solution.py:467
  65.3 32.7 %collective-permute-start.18 = (bf16[512,1024]{1,0:T(8,128)(2,1)S(1)}, bf16[512,1024]{1,0:T(8,128)(2,1)S(1)}, u32[]{:S(2)}, u32[]{:S(2)}) collective-permute-start(bf16[512,1024]{1,0:T(8,128)(2,1)S(1)} %collective-permute-done.17.refs_2_), channel_id=1, source_target_pairs={{4,8},{8,12},{5,9},{9,13},{6,10},{10,14},{7,11},{11,15},{20,24},{2... | collective-permute-start | bytes 3145736 | tf_op jit(solution)/shard_map/ppermute | solution.py:466
  72.1 63.1 %collective-permute-start.16 = (bf16[1024,768]{1,0:T(8,128)(2,1)S(1)}, bf16[1024,768]{1,0:T(8,128)(2,1)S(1)}, u32[]{:S(2)}, u32[]{:S(2)}) collective-permute-start(bf16[1024,768]{1,0:T(8,128)(2,1)S(1)} %shard_map.89.own), channel_id=1, source_target_pairs={{1,0},{3,2},{4,5},{6,7},{9,8},{11,10},{12,13},{14,15},{17,16},{19,... | collective-permute-start | bytes 4718600 | tf_op jit(solution)/shard_map/ppermute | solution.py:443
  75.4 58.4 %collective-permute-start.5 = (bf16[512,1024]{1,0:T(8,128)(2,1)S(1)}, bf16[512,1024]{1,0:T(8,128)(2,1)S(1)}, u32[]{:S(2)}, u32[]{:S(2)}) collective-permute-start(bf16[512,1024]{1,0:T(8,128)(2,1)S(1)} %get-tuple-element.22.own.refs_0_), channel_id=1, source_target_pairs={{0,1},{1,0},{2,3},{3,2},{4,5},{5,4},{6,7},{7,6},{8,9},{9,8},{10,11... | collective-permute-start | bytes 3145736 | tf_op jit(solution)/shard_map/ppermute | solution.py:443
  100.3 36.1 %collective-permute-start.19 = (bf16[1024,512]{1,0:T(8,128)(2,1)S(1)}, bf16[1024,512]{1,0:T(8,128)(2,1)S(1)}, u32[]{:S(2)}, u32[]{:S(2)}) collective-permute-start(bf16[1024,512]{1,0:T(8,128)(2,1)S(1)} %shard_map.91.two), channel_id=1, source_target_pairs={{1,0},{3,2},{4,5},{6,7},{9,8},{11,10},{12,13},{14,15},{17,16},{19,... | collective-permute-start | bytes 3145736 | tf_op jit(solution)/shard_map/ppermute | solution.py:443
  108.1 22.3 %collective-permute-start.8 = (bf16[256,1024]{1,0:T(8,128)(2,1)S(1)}, bf16[256,1024]{1,0:T(8,128)(2,1)S(1)}, u32[]{:S(2)}, u32[]{:S(2)}) collective-permute-start(bf16[256,1024]{1,0:T(8,128)(2,1)S(1)} %collective-permute-done.7.refs_3_), channel_id=1, source_target_pairs={{4,8},{8,12},{5,9},{9,13},{6,10},{10,14},{7,11},{11,15},{20,24},{2... | collective-permute-start | bytes 1572872 | tf_op jit(solution)/shard_map/ppermute | solution.py:466
  109.6 29.8 %collective-permute-start.6 = (bf16[512,1024]{1,0:T(8,128)(2,1)S(1)}, bf16[512,1024]{1,0:T(8,128)(2,1)S(1)}, u32[]{:S(2)}, u32[]{:S(2)}) collective-permute-start(bf16[512,1024]{1,0:T(8,128)(2,1)S(1)} %collective-permute-done.4.other.refs_1_), channel_id=1, source_target_pairs={{0,1},{1,0},{2,3},{3,2},{4,5},{5,4},{6,7},{7,6},{8,9},{9,8},{10,11... | collective-permute-start | bytes 3145736 | tf_op jit(solution)/shard_map/ppermute | solution.py:443
  130.4 42.6 %collective-permute-start.26 = (bf16[1024,768]{1,0:T(8,128)(2,1)S(1)}, bf16[1024,768]{1,0:T(8,128)(2,1)S(1)}, u32[]{:S(2)}, u32[]{:S(2)}) collective-permute-start(bf16[1024,768]{1,0:T(8,128)(2,1)S(1)} %get-tuple-element.34), channel_id=1, source_target_pairs={{3,1},{6,4},{4,6},{11,9},{9,11},{12,14},{19,17},{22,20},{20,22},{2... | collective-permute-start | bytes 4718600 | tf_op jit(solution)/shard_map/ppermute | solution.py:443
  133.9 14.2 %collective-permute-start.29 = (bf16[256,1024]{1,0:T(8,128)(2,1)S(1)}, bf16[256,1024]{1,0:T(8,128)(2,1)S(1)}, u32[]{:S(2)}, u32[]{:S(2)}) collective-permute-start(bf16[256,1024]{1,0:T(8,128)(2,1)S(1)} %get-tuple-element.27.refs_2_), channel_id=1, source_target_pairs={{4,1},{6,3},{9,12},{11,14},{20,17},{22,19},{25,28},{27,30}} | collective-permute-start | bytes 1572872 | tf_op jit(solution)/shard_map/ppermute | solution.py:483
  135.2 16.7 %collective-permute-start.28 = (bf16[256,1024]{1,0:T(8,128)(2,1)S(1)}, bf16[256,1024]{1,0:T(8,128)(2,1)S(1)}, u32[]{:S(2)}, u32[]{:S(2)}) collective-permute-start(bf16[256,1024]{1,0:T(8,128)(2,1)S(1)} %get-tuple-element.27.refs_2_), channel_id=1, source_target_pairs={{5,1},{7,3},{8,12},{10,14},{21,17},{23,19},{24,28},{26,30}} | collective-permute-start | bytes 1572872 | tf_op jit(solution)/shard_map/ppermute | solution.py:483
  136.5 22.8 %collective-permute-start.33 = (bf16[256,1024]{1,0:T(8,128)(2,1)S(1)}, bf16[256,1024]{1,0:T(8,128)(2,1)S(1)}, u32[]{:S(2)}, u32[]{:S(2)}) collective-permute-start(bf16[256,1024]{1,0:T(8,128)(2,1)S(1)} %get-tuple-element.28.refs_3_), channel_id=1, source_target_pairs={{4,1},{6,3},{9,12},{11,14},{20,17},{22,19},{25,28},{27,30}} | collective-permute-start | bytes 1572872 | tf_op jit(solution)/shard_map/ppermute | solution.py:483
  139.4 22.5 %collective-permute-start.32 = (bf16[256,1024]{1,0:T(8,128)(2,1)S(1)}, bf16[256,1024]{1,0:T(8,128)(2,1)S(1)}, u32[]{:S(2)}, u32[]{:S(2)}) collective-permute-start(bf16[256,1024]{1,0:T(8,128)(2,1)S(1)} %get-tuple-element.28.refs_3_), channel_id=1, source_target_pairs={{5,1},{7,3},{8,12},{10,14},{21,17},{23,19},{24,28},{26,30}} | collective-permute-start | bytes 1572872 | tf_op jit(solution)/shard_map/ppermute | solution.py:483
  148.1 27.1 %collective-permute-start.20 = (bf16[1024,512]{1,0:T(8,128)(2,1)S(1)}, bf16[1024,512]{1,0:T(8,128)(2,1)S(1)}, u32[]{:S(2)}, u32[]{:S(2)}) collective-permute-start(bf16[1024,512]{1,0:T(8,128)(2,1)S(1)} %get-tuple-element.30), channel_id=1, source_target_pairs={{0,2},{2,0},{5,7},{7,5},{10,8},{8,10},{15,13},{13,15},{16,18},{18,... | collective-permute-start | bytes 3145736 | tf_op jit(solution)/shard_map/ppermute | solution.py:443
  151.9 11.4 %collective-permute-start.22 = (bf16[1024,256]{1,0:T(8,128)(2,1)S(1)}, bf16[1024,256]{1,0:T(8,128)(2,1)S(1)}, u32[]{:S(2)}, u32[]{:S(2)}) collective-permute-start(bf16[1024,256]{1,0:T(8,128)(2,1)S(1)} %shard_map.94.two), channel_id=1, source_target_pairs={{1,0},{3,2},{4,5},{6,7},{9,8},{11,10},{12,13},{14,15},{17,16},{19,... | collective-permute-start | bytes 1572872 | tf_op jit(solution)/shard_map/ppermute | solution.py:443
  159.3 11.6 %collective-permute-start.12 = (bf16[256,1024]{1,0:T(8,128)(2,1)S(1)}, bf16[256,1024]{1,0:T(8,128)(2,1)S(1)}, u32[]{:S(2)}, u32[]{:S(2)}) collective-permute-start(bf16[256,1024]{1,0:T(8,128)(2,1)S(1)} %shard_map.87.refs_2_), channel_id=1, source_target_pairs={{4,1},{6,3},{9,12},{11,14},{20,17},{22,19},{25,28},{27,30}} | collective-permute-start | bytes 1572872 | tf_op jit(solution)/shard_map/ppermute | solution.py:483
  161.9 12.6 %collective-permute-start.30 = (bf16[1024,256]{1,0:T(8,128)(2,1)S(1)}, bf16[1024,256]{1,0:T(8,128)(2,1)S(1)}, u32[]{:S(2)}, u32[]{:S(2)}) collective-permute-start(bf16[1024,256]{1,0:T(8,128)(2,1)S(1)} %shard_map.100.refs_0_.end_a), channel_id=1, source_target_pairs={{1,3},{14,12},{17,19},{30,28}} | collective-permute-start | bytes 1572872 | tf_op jit(solution)/shard_map/ppermute | solution.py:443
  163.2 15.7 %collective-permute-start.11 = (bf16[256,1024]{1,0:T(8,128)(2,1)S(1)}, bf16[256,1024]{1,0:T(8,128)(2,1)S(1)}, u32[]{:S(2)}, u32[]{:S(2)}) collective-permute-start(bf16[256,1024]{1,0:T(8,128)(2,1)S(1)} %shard_map.87.refs_2_), channel_id=1, source_target_pairs={{5,1},{7,3},{8,12},{10,14},{21,17},{23,19},{24,28},{26,30}} | collective-permute-start | bytes 1572872 | tf_op jit(solution)/shard_map/ppermute | solution.py:483
  170.9 13.7 %collective-permute-start.23 = (bf16[1024,256]{1,0:T(8,128)(2,1)S(1)}, bf16[1024,256]{1,0:T(8,128)(2,1)S(1)}, u32[]{:S(2)}, u32[]{:S(2)}) collective-permute-start(bf16[1024,256]{1,0:T(8,128)(2,1)S(1)} %get-tuple-element.32), channel_id=1, source_target_pairs={{0,2},{2,0},{5,7},{7,5},{10,8},{8,10},{15,13},{13,15},{16,18},{18,... | collective-permute-start | bytes 1572872 | tf_op jit(solution)/shard_map/ppermute | solution.py:443
  174.5 20.2 %collective-permute-start.27 = (bf16[512,768]{1,0:T(8,128)(2,1)S(1)}, bf16[512,768]{1,0:T(8,128)(2,1)S(1)}, u32[]{:S(2)}, u32[]{:S(2)}) collective-permute-start(bf16[512,768]{1,0:T(8,128)(2,1)S(1)} %shard_map.99), channel_id=1, source_target_pairs={{1,17},{4,20},{6,22},{9,25},{11,27},{14,30},{17,1},{20,4},{22,6},{... | collective-permute-start | bytes 2359304 | tf_op jit(solution)/shard_map/ppermute | solution.py:617
  175.2 10.2 %collective-permute-start.36 = (bf16[512,256]{1,0:T(8,128)(2,1)S(1)}, bf16[512,256]{1,0:T(8,128)(2,1)S(1)}, u32[]{:S(2)}, u32[]{:S(2)}) collective-permute-start(bf16[512,256]{1,0:T(8,128)(2,1)S(1)} %get-tuple-element.36), channel_id=1, source_target_pairs={{3,19},{12,28},{19,3},{28,12}} | collective-permute-start | bytes 786440 | tf_op jit(solution)/shard_map/ppermute | solution.py:617
  178.9 9.3 %collective-permute-start.35 = (bf16[512,256]{1,0:T(8,128)(2,1)S(1)}, bf16[512,256]{1,0:T(8,128)(2,1)S(1)}, u32[]{:S(2)}, u32[]{:S(2)}) collective-permute-start(bf16[512,256]{1,0:T(8,128)(2,1)S(1)} %get-tuple-element.36), channel_id=1, source_target_pairs={{1,19},{14,28},{17,3},{30,12}} | collective-permute-start | bytes 786440 | tf_op jit(solution)/shard_map/ppermute | solution.py:617
  181.2 9.7 %collective-permute-start.31 = (bf16[512,256]{1,0:T(8,128)(2,1)S(1)}, bf16[512,256]{1,0:T(8,128)(2,1)S(1)}, u32[]{:S(2)}, u32[]{:S(2)}) collective-permute-start(bf16[512,256]{1,0:T(8,128)(2,1)S(1)} %shard_map.101), channel_id=1, source_target_pairs={{3,19},{12,28},{19,3},{28,12}} | collective-permute-start | bytes 786440 | tf_op jit(solution)/shard_map/ppermute | solution.py:617
  184.6 10.1 %collective-permute-start.21 = (bf16[512,512]{1,0:T(8,128)(2,1)S(1)}, bf16[512,512]{1,0:T(8,128)(2,1)S(1)}, u32[]{:S(2)}, u32[]{:S(2)}) collective-permute-start(bf16[512,512]{1,0:T(8,128)(2,1)S(1)} %shard_map.93), channel_id=1, source_target_pairs={{2,18},{7,23},{8,24},{13,29},{18,2},{23,7},{24,8},{29,13}} | collective-permute-start | bytes 1572872 | tf_op jit(solution)/shard_map/ppermute | solution.py:617
  188.2 8.9 %collective-permute-start.13 = (bf16[512,256]{1,0:T(8,128)(2,1)S(1)}, bf16[512,256]{1,0:T(8,128)(2,1)S(1)}, u32[]{:S(2)}, u32[]{:S(2)}) collective-permute-start(bf16[512,256]{1,0:T(8,128)(2,1)S(1)} %get-tuple-element.24.kept), channel_id=1, source_target_pairs={{1,3},{14,12},{17,19},{30,28}} | collective-permute-start | bytes 786440 | tf_op jit(solution)/shard_map/ppermute | solution.py:443
  193.4 9.2 %collective-permute-start.14 = (bf16[512,256]{1,0:T(8,128)(2,1)S(1)}, bf16[512,256]{1,0:T(8,128)(2,1)S(1)}, u32[]{:S(2)}, u32[]{:S(2)}) collective-permute-start(bf16[512,256]{1,0:T(8,128)(2,1)S(1)} %get-tuple-element.25), channel_id=1, source_target_pairs={{1,19},{14,28},{17,3},{30,12}} | collective-permute-start | bytes 786440 | tf_op jit(solution)/shard_map/ppermute | solution.py:617
  (12 other events, 72.7 us)
